TPU v7x, 32 devices: a whole 2x2x4 slice. The times are simulated.
32 devices in a mesh: dp: 16 (over z, x, core), seq: 2 (over y).
Axes of the slice: x: 2, y: 2, z: 4, core: 2. Of those that a mesh axis runs over, the one named last changes fastest.
Arguments:
- tokens: bfloat16 [24576, 768], P(('dp', 'seq')), may hold values from -7 to 7
- entity_flags: int32 [24576], P(('dp', 'seq')), may hold values 0 or 1
- query_weight: bfloat16 [4, 768, 768], P(None, 'dp'), may hold values from -0.21875 to 0.21875
- key_weight: bfloat16 [768, 768], P('dp'), may hold values from -0.21875 to 0.21875
- value_weight: bfloat16 [768, 768], P('dp'), may hold values from -0.21875 to 0.21875
- mixing_weight: bfloat16 [768, 768], P('dp'), may hold values from -4 to 4
- mixing_bias: bfloat16 [768], P('dp'), may hold values from -4 to 4
- first_gain: bfloat16 [768], P('dp'), may hold values from 0.5 to 1.5
- first_bias: bfloat16 [768], P('dp'), may hold values from -4 to 4
- up_weight: bfloat16 [768, 3072], P('dp'), may hold values from -0.21875 to 0.21875
- up_bias: bfloat16 [3072], P('dp'), may hold values from -4 to 4
- down_weight: bfloat16 [3072, 768], P('dp'), may hold values from -0.109375 to 0.109375
- down_bias: bfloat16 [768], P('dp'), may hold values from -4 to 4
- second_gain: bfloat16 [768], P('dp'), may hold values from 0.5 to 1.5
- second_bias: bfloat16 [768], P('dp'), may hold values from -4 to 4
- cotangent: bfloat16 [24576, 768], P(('dp', 'seq')), may hold values from -6 to 6
Outputs:
- layer_out: bfloat16 [24576, 768], P(('dp', 'seq'))
- tokens_grad: bfloat16 [24576, 768], P(('dp', 'seq'))
- query_grad: float32 [4, 768, 768], P(None, 'dp')
- key_grad: float32 [768, 768], P('dp')
- value_grad: float32 [768, 768], P('dp')
- mixing_grad: float32 [768, 768], P('dp')
- mixing_bias_grad: float32 [768], P('dp')
- first_gain_grad: float32 [768], P('dp')
- first_bias_grad: float32 [768], P('dp')
- up_grad: float32 [768, 3072], P('dp')
- up_bias_grad: float32 [3072], P('dp')
- down_grad: float32 [3072, 768], P('dp')
- down_bias_grad: float32 [768], P('dp')
- second_gain_grad: float32 [768], P('dp')
- second_bias_grad: float32 [768], P('dp')
- stream_rms: float32 [3], replicated
All inputs are finite; a program needn't handle non-finite values. No bound on the sum of `entity_flags` on one device may be relied on, other than what follows from the above.
Results may differ from a plain program's by a relative error of at most 0.015.
Values may be sent and summed in bfloat16 or wider, within the bound.
No kernel may reach another device: no remote copies, remote signals or barrier semaphores. Data moves between devices by JAX's collectives and lax.ppermute only.
A program may use at most 192 MiB of HBM per device.

v0:
```python
import jax
import jax.numpy as jnp
from jax import lax
from jax.sharding import PartitionSpec as P

D = 768
HEADS = 12
HD = 64


epsilon = 1e-05


def matmul(left, right):
    return jnp.dot(left, right, preferred_element_type=jnp.float32)


def transposed_left(left, right):
    return lax.dot_general(
        left, right, (((0,), (0,)), ((), ())), preferred_element_type=jnp.float32
    )


def transposed_right(left, right):
    return lax.dot_general(
        left, right, (((1,), (1,)), ((), ())), preferred_element_type=jnp.float32
    )


def layer_norm(value, gain, shift):
    center = value - jnp.mean(value, axis=-1, keepdims=True)
    inverse = lax.rsqrt(jnp.mean(center * center, axis=-1, keepdims=True) + epsilon)
    normed = center * inverse
    return (normed * gain + shift, normed, inverse)


def norm_backward(upstream, normed, inverse, gain):
    scaled = upstream * gain
    row_inner = (
        scaled
        - jnp.mean(scaled, axis=-1, keepdims=True)
        - normed * jnp.mean(scaled * normed, axis=-1, keepdims=True)
    )
    return (row_inner * inverse, jnp.sum(upstream * normed, axis=0), jnp.sum(upstream, axis=0))


def gelu_exact(value):
    return 0.5 * value * (1.0 + lax.erf(value * 0.7071067811865476))


def gelu_slope(value):
    return (
        0.5 * (1.0 + lax.erf(value * 0.7071067811865476))
        + value * jnp.exp(-0.5 * value * value) * 0.3989422804014327
    )


def pair_slices(queries, keys_masked, values, pair_index, length):
    pair_width = 4 * HD
    query_pair = lax.dynamic_slice_in_dim(queries, pair_index * pair_width, pair_width, 1).reshape(
        length, 2, 2 * HD
    )
    key_pair = lax.dynamic_slice_in_dim(
        keys_masked, pair_index * pair_width, pair_width, 1
    ).reshape(length, 2, 2 * HD)
    value_pair = lax.dynamic_slice_in_dim(values, pair_index * 2 * HD, 2 * HD, 1).reshape(
        length, 2, HD
    )
    return (query_pair, key_pair, value_pair)


def attend_forward(queries, keys_masked, values, head_count):
    length = queries.shape[0]
    block_rows = min(512, length)
    score_scale = HD ** (-0.5)

    def pair_work(pair_index):
        query_pair, key_pair, value_pair = pair_slices(
            queries, keys_masked, values, pair_index, length
        )

        def block_work(block_index):
            query_block = lax.dynamic_slice_in_dim(
                query_pair, block_index * block_rows, block_rows, 0
            )
            scores = score_scale * jnp.einsum(
                "qhc,khc->hqk", query_block, key_pair, preferred_element_type=jnp.float32
            )
            highest = jnp.max(scores, axis=-1, keepdims=True)
            weights = jnp.exp(scores - highest)
            totals = jnp.sum(weights, axis=-1, keepdims=True)
            weights_low = (weights / totals).astype(jnp.bfloat16)
            mixture = jnp.einsum(
                "hqk,khc->qhc", weights_low, value_pair, preferred_element_type=jnp.float32
            )
            return (
                mixture.astype(jnp.bfloat16).reshape(block_rows, 2 * HD),
                (highest + jnp.log(totals))[:, :, 0],
            )

        mixture, logsum = lax.map(block_work, jnp.arange(length // block_rows))
        return (mixture.reshape(length, 2 * HD), logsum)

    mixture, logsum = lax.map(pair_work, jnp.arange(head_count // 2))
    return (jnp.transpose(mixture, (1, 0, 2)).reshape(length, head_count * HD), logsum)


def attend_backward(queries, keys_masked, values, grad_mixture, logsum, head_count):
    length = queries.shape[0]
    block_rows = min(512, length)
    score_scale = HD ** (-0.5)

    def pair_work(pair_index):
        query_pair, key_pair, value_pair = pair_slices(
            queries, keys_masked, values, pair_index, length
        )
        grad_pair = lax.dynamic_slice_in_dim(grad_mixture, pair_index * 2 * HD, 2 * HD, 1).reshape(
            length, 2, HD
        )
        pair_logsum = logsum[pair_index]

        def block_work(running, block_index):
            key_sum, value_sum = running
            query_block = lax.dynamic_slice_in_dim(
                query_pair, block_index * block_rows, block_rows, 0
            )
            grad_block = lax.dynamic_slice_in_dim(
                grad_pair, block_index * block_rows, block_rows, 0
            )
            scores = score_scale * jnp.einsum(
                "qhc,khc->hqk", query_block, key_pair, preferred_element_type=jnp.float32
            )
            weights = jnp.exp(scores - pair_logsum[block_index][:, :, None])
            weight_grad = jnp.einsum(
                "qhc,khc->hqk", grad_block, value_pair, preferred_element_type=jnp.float32
            )
            row_inner = jnp.sum(weights * weight_grad, axis=-1, keepdims=True)
            score_grad = (weights * (weight_grad - row_inner)).astype(jnp.bfloat16)
            query_part = score_scale * jnp.einsum(
                "hqk,khc->qhc", score_grad, key_pair, preferred_element_type=jnp.float32
            )
            key_sum = key_sum + score_scale * jnp.einsum(
                "hqk,qhc->khc", score_grad, query_block, preferred_element_type=jnp.float32
            )
            value_sum = value_sum + jnp.einsum(
                "hqk,qhc->khc",
                weights.astype(jnp.bfloat16),
                grad_block,
                preferred_element_type=jnp.float32,
            )
            return (
                (key_sum, value_sum),
                query_part.astype(jnp.bfloat16).reshape(block_rows, 4 * HD),
            )

        start_sums = (
            jnp.zeros((length, 2, 2 * HD), jnp.float32),
            jnp.zeros((length, 2, HD), jnp.float32),
        )
        (key_sum, value_sum), query_part = lax.scan(
            block_work, start_sums, jnp.arange(length // block_rows)
        )
        return (
            query_part.reshape(length, 4 * HD),
            key_sum.astype(jnp.bfloat16).reshape(length, 4 * HD),
            value_sum.astype(jnp.bfloat16).reshape(length, 2 * HD),
        )

    query_part, key_part, value_part = lax.map(pair_work, jnp.arange(head_count // 2))
    return (
        jnp.transpose(query_part, (1, 0, 2)).reshape(length, head_count * 2 * HD),
        jnp.transpose(key_part, (1, 0, 2)).reshape(length, head_count * 2 * HD),
        jnp.transpose(value_part, (1, 0, 2)).reshape(length, head_count * HD),
    )


def local(
    tokens,
    entity_flags,
    query_weight,
    key_weight,
    value_weight,
    mixing_weight,
    mixing_bias,
    first_gain,
    first_bias,
    up_weight,
    up_bias,
    down_weight,
    down_bias,
    second_gain,
    second_bias,
    cotangent,
):
    (
        query_full,
        key_full,
        value_full,
        mixing_full,
        mixing_shift,
        gain_one,
        shift_one,
        up_full,
        up_shift,
        down_full,
        down_shift,
        gain_two,
        shift_two,
    ) = (
        lax.all_gather(query_weight, "dp", axis=1, tiled=True),
        lax.all_gather(key_weight, "dp", axis=0, tiled=True),
        lax.all_gather(value_weight, "dp", axis=0, tiled=True),
        lax.all_gather(mixing_weight, "dp", axis=0, tiled=True),
        lax.all_gather(mixing_bias, "dp", axis=0, tiled=True),
        lax.all_gather(first_gain, "dp", axis=0, tiled=True),
        lax.all_gather(first_bias, "dp", axis=0, tiled=True),
        lax.all_gather(up_weight, "dp", axis=0, tiled=True),
        lax.all_gather(up_bias, "dp", axis=0, tiled=True),
        lax.all_gather(down_weight, "dp", axis=0, tiled=True),
        lax.all_gather(down_bias, "dp", axis=0, tiled=True),
        lax.all_gather(second_gain, "dp", axis=0, tiled=True),
        lax.all_gather(second_bias, "dp", axis=0, tiled=True),
    )
    row_count = tokens.shape[0]
    seq_count = lax.axis_size("seq")
    head_count = HEADS // seq_count
    entity = entity_flags.astype(jnp.float32)[:, None]
    wordly = 1.0 - entity
    projected = jnp.einsum("td,mde->tme", tokens, query_full, preferred_element_type=jnp.float32)
    to_word = wordly * projected[:, 0] + entity * projected[:, 2]
    to_entity = wordly * projected[:, 1] + entity * projected[:, 3]
    key_rows = matmul(tokens, key_full)
    queries = (
        jnp.stack(
            [to_word.reshape(row_count, HEADS, HD), to_entity.reshape(row_count, HEADS, HD)], axis=2
        )
        .astype(jnp.bfloat16)
        .reshape(row_count, 2 * D)
    )
    values = matmul(tokens, value_full).astype(jnp.bfloat16)
    keys_masked = (
        jnp.stack(
            [
                (wordly * key_rows).reshape(row_count, HEADS, HD),
                (entity * key_rows).reshape(row_count, HEADS, HD),
            ],
            axis=2,
        )
        .astype(jnp.bfloat16)
        .reshape(row_count, 2 * D)
    )
    head_queries, head_keys, head_values = (
        lax.all_to_all(queries, "seq", split_axis=1, concat_axis=0, tiled=True),
        lax.all_to_all(keys_masked, "seq", split_axis=1, concat_axis=0, tiled=True),
        lax.all_to_all(values, "seq", split_axis=1, concat_axis=0, tiled=True),
    )
    head_mixture, logsum = attend_forward(head_queries, head_keys, head_values, head_count)
    mixture = lax.all_to_all(head_mixture, "seq", split_axis=0, concat_axis=1, tiled=True)
    attention_out = matmul(mixture, mixing_full) + mixing_shift.astype(jnp.float32)
    stream = tokens.astype(jnp.float32) + attention_out
    hidden, normed_one, inverse_one = layer_norm(
        stream, gain_one.astype(jnp.float32), shift_one.astype(jnp.float32)
    )
    hidden_low = hidden.astype(jnp.bfloat16)
    before = matmul(hidden_low, up_full) + up_shift.astype(jnp.float32)
    active = gelu_exact(before).astype(jnp.bfloat16)
    forward_out = matmul(active, down_full) + down_shift.astype(jnp.float32)
    layer_out, normed_two, inverse_two = layer_norm(
        hidden + forward_out, gain_two.astype(jnp.float32), shift_two.astype(jnp.float32)
    )
    squares = jnp.stack(
        [
            jnp.sum(stream * stream),
            jnp.sum(attention_out * attention_out),
            jnp.sum(forward_out * forward_out),
        ]
    )
    totals = lax.psum(squares, ("dp", "seq"))
    stream_rms = jnp.sqrt(totals / (row_count * lax.axis_size("dp") * seq_count * D))
    (
        query_back,
        key_back,
        value_back,
        mixing_back,
        gain_back_one,
        up_back,
        down_back,
        gain_back_two,
    ) = (
        lax.all_gather(query_weight, "dp", axis=1, tiled=True),
        lax.all_gather(key_weight, "dp", axis=0, tiled=True),
        lax.all_gather(value_weight, "dp", axis=0, tiled=True),
        lax.all_gather(mixing_weight, "dp", axis=0, tiled=True),
        lax.all_gather(first_gain, "dp", axis=0, tiled=True),
        lax.all_gather(up_weight, "dp", axis=0, tiled=True),
        lax.all_gather(down_weight, "dp", axis=0, tiled=True),
        lax.all_gather(second_gain, "dp", axis=0, tiled=True),
    )
    upstream = cotangent.astype(jnp.float32)
    grad_residual, second_gain_sum, second_bias_sum = norm_backward(
        upstream, normed_two, inverse_two, gain_back_two.astype(jnp.float32)
    )
    grad_forward = grad_residual.astype(jnp.bfloat16)
    down_sum = transposed_left(active, grad_forward)
    down_bias_sum = jnp.sum(grad_forward.astype(jnp.float32), axis=0)
    grad_before = (transposed_right(grad_forward, down_back) * gelu_slope(before)).astype(
        jnp.bfloat16
    )
    up_sum = transposed_left(hidden_low, grad_before)
    up_bias_sum = jnp.sum(grad_before.astype(jnp.float32), axis=0)
    grad_hidden = grad_residual + transposed_right(grad_before, up_back)
    grad_stream, first_gain_sum, first_bias_sum = norm_backward(
        grad_hidden, normed_one, inverse_one, gain_back_one.astype(jnp.float32)
    )
    grad_attention = grad_stream.astype(jnp.bfloat16)
    mixing_sum = transposed_left(mixture, grad_attention)
    mixing_bias_sum = jnp.sum(grad_attention.astype(jnp.float32), axis=0)
    grad_mixture = transposed_right(grad_attention, mixing_back).astype(jnp.bfloat16)
    head_grad = lax.all_to_all(grad_mixture, "seq", split_axis=1, concat_axis=0, tiled=True)
    query_part, key_part, value_part = attend_backward(
        head_queries, head_keys, head_values, head_grad, logsum, head_count
    )
    wordly_low = wordly.astype(jnp.bfloat16)
    entity_low = entity.astype(jnp.bfloat16)
    token_queries, token_keys, token_values = (
        lax.all_to_all(query_part, "seq", split_axis=0, concat_axis=1, tiled=True),
        lax.all_to_all(key_part, "seq", split_axis=0, concat_axis=1, tiled=True),
        lax.all_to_all(value_part, "seq", split_axis=0, concat_axis=1, tiled=True),
    )
    split_keys = token_keys.reshape(row_count, HEADS, 2, HD)
    key_token = wordly_low * split_keys[:, :, 0].reshape(row_count, D) + entity_low * split_keys[
        :, :, 1
    ].reshape(row_count, D)
    split_queries = token_queries.reshape(row_count, HEADS, 2, HD)
    grad_word = split_queries[:, :, 0].reshape(row_count, D)
    grad_entity = split_queries[:, :, 1].reshape(row_count, D)
    projected_grad = jnp.stack(
        [
            wordly_low * grad_word,
            wordly_low * grad_entity,
            entity_low * grad_word,
            entity_low * grad_entity,
        ],
        axis=1,
    )
    query_sum = jnp.einsum(
        "td,tme->mde", tokens, projected_grad, preferred_element_type=jnp.float32
    )
    key_sum = transposed_left(tokens, key_token)
    value_sum = transposed_left(tokens, token_values)
    input_grad = (
        grad_stream
        + jnp.einsum("tme,mde->td", projected_grad, query_back, preferred_element_type=jnp.float32)
        + transposed_right(key_token, key_back)
        + transposed_right(token_values, value_back)
    )
    shares = (
        lax.psum_scatter(query_sum, "dp", scatter_dimension=1, tiled=True),
        lax.psum_scatter(key_sum, "dp", scatter_dimension=0, tiled=True),
        lax.psum_scatter(value_sum, "dp", scatter_dimension=0, tiled=True),
        lax.psum_scatter(mixing_sum, "dp", scatter_dimension=0, tiled=True),
        lax.psum_scatter(mixing_bias_sum, "dp", scatter_dimension=0, tiled=True),
        lax.psum_scatter(first_gain_sum, "dp", scatter_dimension=0, tiled=True),
        lax.psum_scatter(first_bias_sum, "dp", scatter_dimension=0, tiled=True),
        lax.psum_scatter(up_sum, "dp", scatter_dimension=0, tiled=True),
        lax.psum_scatter(up_bias_sum, "dp", scatter_dimension=0, tiled=True),
        lax.psum_scatter(down_sum, "dp", scatter_dimension=0, tiled=True),
        lax.psum_scatter(down_bias_sum, "dp", scatter_dimension=0, tiled=True),
        lax.psum_scatter(second_gain_sum, "dp", scatter_dimension=0, tiled=True),
        lax.psum_scatter(second_bias_sum, "dp", scatter_dimension=0, tiled=True),
    )
    reduced = (
        lax.psum(shares[0].astype(jnp.bfloat16), "seq").astype(jnp.float32),
        lax.psum(shares[1].astype(jnp.bfloat16), "seq").astype(jnp.float32),
        lax.psum(shares[2].astype(jnp.bfloat16), "seq").astype(jnp.float32),
        lax.psum(shares[3].astype(jnp.bfloat16), "seq").astype(jnp.float32),
        lax.psum(shares[4].astype(jnp.bfloat16), "seq").astype(jnp.float32),
        lax.psum(shares[5].astype(jnp.bfloat16), "seq").astype(jnp.float32),
        lax.psum(shares[6].astype(jnp.bfloat16), "seq").astype(jnp.float32),
        lax.psum(shares[7].astype(jnp.bfloat16), "seq").astype(jnp.float32),
        lax.psum(shares[8].astype(jnp.bfloat16), "seq").astype(jnp.float32),
        lax.psum(shares[9].astype(jnp.bfloat16), "seq").astype(jnp.float32),
        lax.psum(shares[10].astype(jnp.bfloat16), "seq").astype(jnp.float32),
        lax.psum(shares[11].astype(jnp.bfloat16), "seq").astype(jnp.float32),
        lax.psum(shares[12].astype(jnp.bfloat16), "seq").astype(jnp.float32),
    )
    return (
        layer_out.astype(jnp.bfloat16),
        input_grad.astype(jnp.bfloat16),
        reduced[0],
        reduced[1],
        reduced[2],
        reduced[3],
        reduced[4],
        reduced[5],
        reduced[6],
        reduced[7],
        reduced[8],
        reduced[9],
        reduced[10],
        reduced[11],
        reduced[12],
        stream_rms,
    )


def solution(mesh):
    in_specs = (
        P(("dp", "seq"), None),
        P(("dp", "seq")),
        P(None, "dp", None),
        P("dp", None),
        P("dp", None),
        P("dp", None),
        P("dp"),
        P("dp"),
        P("dp"),
        P("dp", None),
        P("dp"),
        P("dp", None),
        P("dp"),
        P("dp"),
        P("dp"),
        P(("dp", "seq"), None),
    )
    out_specs = (
        P(("dp", "seq"), None),
        P(("dp", "seq"), None),
        P(None, "dp", None),
        P("dp", None),
        P("dp", None),
        P("dp", None),
        P("dp"),
        P("dp"),
        P("dp"),
        P("dp", None),
        P("dp"),
        P("dp", None),
        P("dp"),
        P("dp"),
        P("dp"),
        P(),
    )
    return jax.shard_map(local, mesh=mesh, in_specs=in_specs, out_specs=out_specs, check_vma=False)
```

profile of v0, /device:TPU:0, one launch (start us, length us, event | category | flops | bytes accessed | tf_op | source)
XLA Modules:
  0.0 1261.5 jit_solution(7962755866159456664)
XLA Ops:
  13.1 38.2 %all-gather.11.cloned.1.call-done = bf16[768,768]{1,0:T(8,128)(2,1)} async-done(((bf16[48,768]{1,0:T(8,128)(2,1)}), bf16[768,768]{1,0:T(8,128)(2,1)}) %all-gather.11.cloned.1.call-update) | async-done | bytes 1179664 | tf_op jit(solution)/shard_map/all_gather | solution.py:212
  58.9 32.1 %all-gather.9.cloned.1.call-done = bf16[768,768]{1,0:T(8,128)(2,1)} async-done(((bf16[48,768]{1,0:T(8,128)(2,1)}), bf16[768,768]{1,0:T(8,128)(2,1)}) %all-gather.9.cloned.1.call-update) | async-done | bytes 1179664 | tf_op jit(solution)/shard_map/all_gather | solution.py:211
  95.0 50.5 %all-gather.7.cloned.1.call-done = bf16[4,768,768]{2,1,0:T(8,128)(2,1)} async-done(((bf16[4,48,768]{2,1,0:T(8,128)(2,1)}), bf16[4,768,768]{2,1,0:T(8,128)(2,1)}) %all-gather.7.cloned.1.call-update) | async-done | bytes 4718608 | tf_op jit(solution)/shard_map/all_gather | solution.py:210
  145.5 10.0 fusion.46
  166.3 21.3 %all-to-all-done.1 = bf16[768,2,768]{0,2,1:T(8,128)(2,1)S(1)} async-done(((bf16[768,2,768]{0,2,1:T(8,128)(2,1)}), bf16[768,2,768]{0,2,1:T(8,128)(2,1)S(1)}, u32[]{:S(2)}, u32[]{:S(2)}) %all-to-all-start.1) | async-done | bytes 2359328 | tf_op jit(solution)/shard_map/all_to_all | solution.py:254
  201.0 19.1 %all-to-all-done = bf16[768,2,768]{0,2,1:T(8,128)(2,1)} async-done(((bf16[768,2,768]{0,2,1:T(8,128)(2,1)}), bf16[768,2,768]{0,2,1:T(8,128)(2,1)}, u32[]{:S(2)}, u32[]{:S(2)}) %all-to-all-start) | async-done | bytes 2359328 | tf_op jit(solution)/shard_map/all_to_all | solution.py:253
  225.5 68.6 %while.85 = (s32[]{:T(128)}, bf16[3,1536,128]{2,1,0:T(8,128)(2,1)}, f32[3,3,2,512]{3,2,1,0:T(2,128)}, s32[3]{0:T(128)S(1)}, bf16[1536,768]{0,1:T(8,128)(2,1)}, /...) while((s32[]{:T(128)}, bf16[3,1536,128]{2,1,0:T(8,128)(2,1)}, ...), condition=%wide.region_5.6_spmd, body=%wide.region_0.5_spmd.sunk | while | flops 618200064 | bytes 27321900 | solution.py:104
  230.3 16.7 %while.88 = (s32[]{:T(128)}, bf16[3,512,128]{2,1,0:T(8,128)(2,1)S(1)}, f32[3,2,512]{2,1,0:T(2,128)S(1)}, s32[3]{0:T(128)S(1)}, bf16[1536,2,128]{0,2,1:T(8,128)(2...) while((s32[]{:T(128)}, ...), condition=%wide.region_4.4_spmd, body=%wide.region_1.3_spmd.sunk | while | flops 618200064 | bytes 21004468 | solution.py:101
  253.2 16.6 %while.88 = (s32[]{:T(128)}, bf16[3,512,128]{2,1,0:T(8,128)(2,1)S(1)}, f32[3,2,512]{2,1,0:T(2,128)S(1)}, s32[3]{0:T(128)S(1)}, bf16[1536,2,128]{0,2,1:T(8,128)(2...) while((s32[]{:T(128)}, ...), condition=%wide.region_4.4_spmd, body=%wide.region_1.3_spmd.sunk | while | flops 618200064 | bytes 21004468 | solution.py:101
  276.1 16.6 %while.88 = (s32[]{:T(128)}, bf16[3,512,128]{2,1,0:T(8,128)(2,1)S(1)}, f32[3,2,512]{2,1,0:T(2,128)S(1)}, s32[3]{0:T(128)S(1)}, bf16[1536,2,128]{0,2,1:T(8,128)(2...) while((s32[]{:T(128)}, ...), condition=%wide.region_4.4_spmd, body=%wide.region_1.3_spmd.sunk | while | flops 618200064 | bytes 21004468 | solution.py:101
  308.4 57.9 %all-reduce.16 = (bf16[768]{0:T(1024)(128)(2,1)S(1)}, bf16[768]{0:T(1024)(128)(2,1)S(1)}, bf16[768]{0:T(1024)(128)(2,1)S(1)}, bf16[3072]{0:T(1024)(128)(2,1)S(1)...) all-reduce(bf16[768]{0:T(1024)(128)(2,1)S(1)} %dynamic-update-slice, ...), channel_id=1, replica_groups=mesh['dp'=16,'seq'=2] {'dp'}, use_global_device_ids=true, to_apply=%add | all-reduce | flops 7680 | bytes 30720
  374.8 10.7 multiply_convert_fusion.1
  385.5 8.7 fusion.60
  398.9 10.9 convert_reduce_fusion
  409.8 5.9 multiply_reduce_fusion.5
  427.2 7.2 all-to-all-done.4
  436.7 281.8 %while.87 = (s32[]{:T(128)}, bf16[3,1536,256]{2,1,0:T(8,128)(2,1)}, bf16[3,1536,256]{1,2,0:T(8,128)(2,1)}, bf16[3,1536,128]{1,2,0:T(8,128)(2,1)}, s32[3]{0:T(128...) while((s32[]{:T(128)}, bf16[3,1536,256]{2,1,0:T(8,128)(2,1)}, ...), condition=%wide.region_18.19_spmd, body=%wide.region_14.18_spmd.sunk | while | flops 1625619456 | bytes 143703296 | solution.py:169
  444.2 82.3 %while.89 = (s32[]{:T(128)}, f32[1536,2,128]{0,2,1:T(8,128)}, f32[1536,2,64]{0,2,1:T(8,128)}, bf16[3,512,256]{2,1,0:T(8,128)(2,1)}, s32[3]{0:T(128)S(1)}, /*inde...) while((s32[]{:T(128)}, f32[1536,2,128]{0,2,1:T(8,128)}, ...), condition=%wide.region_17.17_spmd.clone, body=%wide.region_15.16_spmd.clone.sunk | while | flops 1625029632 | bytes 115758232 | solution.py:160
  538.0 82.2 %while.89 = (s32[]{:T(128)}, f32[1536,2,128]{0,2,1:T(8,128)}, f32[1536,2,64]{0,2,1:T(8,128)}, bf16[3,512,256]{2,1,0:T(8,128)(2,1)}, s32[3]{0:T(128)S(1)}, /*inde...) while((s32[]{:T(128)}, f32[1536,2,128]{0,2,1:T(8,128)}, ...), condition=%wide.region_17.17_spmd.clone, body=%wide.region_15.16_spmd.clone.sunk | while | flops 1625029632 | bytes 115758232 | solution.py:160
  632.0 82.2 %while.89 = (s32[]{:T(128)}, f32[1536,2,128]{0,2,1:T(8,128)}, f32[1536,2,64]{0,2,1:T(8,128)}, bf16[3,512,256]{2,1,0:T(8,128)(2,1)}, s32[3]{0:T(128)S(1)}, /*inde...) while((s32[]{:T(128)}, f32[1536,2,128]{0,2,1:T(8,128)}, ...), condition=%wide.region_17.17_spmd.clone, body=%wide.region_15.16_spmd.clone.sunk | while | flops 1625029632 | bytes 115758232 | solution.py:160
  721.6 12.9 %all_to_all.140 = bf16[2,768,384]{1,2,0:T(8,128)(2,1)S(1)} all-to-all(bf16[2,768,384]{1,2,0:T(8,128)(2,1)S(1)} %copy.176), channel_id=1, replica_groups=mesh['dp'=16,'seq'=2] {'seq'}, dimensions={0} | all-to-all | bytes 2359296 | tf_op jit(solution)/shard_map/all_to_all | solution.py:328
  743.9 24.5 %all_to_all.141 = bf16[2,768,768]{1,2,0:T(8,128)(2,1)S(1)} all-to-all(bf16[2,768,768]{1,2,0:T(8,128)(2,1)S(1)} %copy.174), channel_id=1, replica_groups=mesh['dp'=16,'seq'=2] {'seq'}, dimensions={0} | all-to-all | bytes 4718592 | tf_op jit(solution)/shard_map/all_to_all | solution.py:327
  775.2 9.1 fusion.55
  785.6 8.8 fusion.66
  810.2 67.0 %psum.111 = f32[3]{0:T(128)S(1)} all-reduce(f32[3]{0:T(128)S(1)} %pad_maximum_fusion.5), channel_id=1, replica_groups=mesh['dp'=16,'seq'=2] {'dp','seq'}, use_global_device_ids=true, to_apply=%region_55.56 | all-reduce | flops 3 | bytes 24 | tf_op jit(solution)/shard_map/psum | solution.py:278
  889.7 6.4 convolution_bitcast_fusion
  896.2 12.2 copy.179
  908.4 252.6 %all-reduce.23 = (bf16[4,768,768]{2,0,1:T(4,128)(2,1)}, bf16[768]{0:T(1024)(128)(2,1)S(1)}, bf16[768]{0:T(1024)(128)(2,1)S(1)}, bf16[768]{0:T(1024)(128)(2,1)S(1...) all-reduce(f32[4,768,768]{2,0,1:T(4,128)} %copy.179, ...), channel_id=2, replica_groups=mesh['dp'=16,'seq'=2] {'dp'}, use_global_device_ids=true, to_apply=%region_19.20.clone | all-reduce | flops 2366976 | bytes 14201856
  1161.5 5.2 all-reduce.17
  1181.7 7.8 reduce-scatter.14.cloned.1.call-done
  1191.3 9.0 fusion.42
  1201.7 44.9 %all-reduce.22.cloned.1.call-done = (bf16[4,48,768]{2,0,1:T(4,128)(2,1)}, bf16[48,768]{0,1:T(8,128)(2,1)}, bf16[48,768]{0,1:T(8,128)(2,1)}, bf16[48,768]{1,0:T(8...) async-done(((bf16[4,48,768]{2,0,1:T(4,128)(2,1)}, bf16[48,768]{0,1:T(8,128)(2,1)}, bf16[48,768]{0,1:T(8,128)(2,1)}, bf16[48,768]{1,0:T(8,128)(2,1)}, ...) | async-done | bytes 1105936 | tf_op jit(solution)/shard_map/psum | solution.py:373
  (711 shorter events, 465.8 us)
Async XLA Ops:
  7.2 44.2 %all-gather.11.cloned.1.call-start = ((), (), s32[]{:S(2)}) async-start(), calls=%async_computation.15 | async-start | bytes 1253376 | tf_op jit(solution)/shard_map/all_gather | solution.py:212
  7.9 83.0 %all-gather.9.cloned.1.call-start = ((), (), s32[]{:S(2)}) async-start(), calls=%async_computation.14 | async-start | bytes 1253376 | tf_op jit(solution)/shard_map/all_gather | solution.py:211
  8.7 136.8 %all-gather.7.cloned.1.call-start = ((), (), s32[]{:S(2)}) async-start(), calls=%async_computation.13 | async-start | bytes 5013504 | tf_op jit(solution)/shard_map/all_gather | solution.py:210
  9.4 360.0 %all-gather.13.cloned.1.call-start = ((), (), s32[]{:S(2)}) async-start(), calls=%async_computation.16 | async-start | bytes 1253376 | tf_op jit(solution)/shard_map/all_gather | solution.py:213
  10.0 364.8 %all-gather.15.cloned.1.call-start = ((), (), s32[]{:S(2)}) async-start(), calls=%async_computation.17 | async-start | bytes 5013504 | tf_op jit(solution)/shard_map/all_gather | solution.py:217
  55.1 35.8 %copy-start.22 = (bf16[768,768]{1,0:T(8,128)(2,1)S(1)}, bf16[768,768]{1,0:T(8,128)(2,1)}, u32[]{:S(2)}) copy-start(bf16[768,768]{1,0:T(8,128)(2,1)} %param.24) | copy-start | bytes 3538948
  55.1 100.4 %all-to-all-start.2 = ((bf16[768,2,384]{0,2,1:T(8,128)(2,1)}), bf16[768,2,384]{0,2,1:T(8,128)(2,1)S(1)}, u32[]{:S(2)}, u32[]{:S(2)}) async-start(bf16[768,2,384]{0,2,1:T(8,128)(2,1)} %bitcast.39), calls=%async_computation.2 | async-start | bytes 2359296 | tf_op jit(solution)/shard_map/all_to_all | solution.py:255
  155.5 32.1 %all-to-all-start.1 = ((bf16[768,2,768]{0,2,1:T(8,128)(2,1)}), bf16[768,2,768]{0,2,1:T(8,128)(2,1)S(1)}, u32[]{:S(2)}, u32[]{:S(2)}) async-start(bf16[768,2,768]{0,2,1:T(8,128)(2,1)} %bitcast.254), calls=%async_computation.1 | async-start | bytes 4718592 | tf_op jit(solution)/shard_map/all_to_all | solution.py:254
  187.6 32.5 %all-to-all-start = ((bf16[768,2,768]{0,2,1:T(8,128)(2,1)}), bf16[768,2,768]{0,2,1:T(8,128)(2,1)}, u32[]{:S(2)}, u32[]{:S(2)}) async-start(bf16[768,2,768]{0,2,1:T(8,128)(2,1)} %bitcast.255), calls=%async_computation | async-start | bytes 4718592 | tf_op jit(solution)/shard_map/all_to_all | solution.py:253
  192.5 193.0 %all-gather.17.cloned.1.call-start = ((), (), s32[]{:S(2)}) async-start(), calls=%async_computation.18 | async-start | bytes 5013504 | tf_op jit(solution)/shard_map/all_gather | solution.py:219
  297.2 70.9 %copy-start.21 = (bf16[768,768]{1,0:T(8,128)(2,1)S(1)}, bf16[768,768]{1,0:T(8,128)(2,1)}, u32[]{:S(2)}) copy-start(bf16[768,768]{1,0:T(8,128)(2,1)} %param.39) | copy-start | bytes 3538948
  297.2 72.2 %all-to-all-start.3 = ((bf16[2,768,384]{1,2,0:T(8,128)(2,1)}), bf16[2,768,384]{1,2,0:T(8,128)(2,1)S(1)}, u32[]{:S(2)}, u32[]{:S(2)}) async-start(bf16[2,768,384]{1,2,0:T(8,128)(2,1)} %copy.159), calls=%async_computation.3 | async-start | bytes 2359296 | tf_op jit(solution)/shard_map/all_to_all | solution.py:258
  366.3 49.4 %copy-start.42 = (f32[768]{0:T(1024)}, f32[768]{0:T(1024)S(1)}, u32[]{:S(2)}) copy-start(f32[768]{0:T(1024)S(1)} %convert_element_type.205) | copy-start | bytes 9220
  374.4 41.3 %copy-start.9 = (f32[768,768]{0,1:T(8,128)}, f32[768,768]{0,1:T(8,128)S(1)}, u32[]{:S(2)}) copy-start(f32[768,768]{0,1:T(8,128)S(1)} %get-tuple-element.658) | copy-start | bytes 7077892
  374.5 41.3 %copy-start.36 = (f32[768]{0:T(1024)}, f32[768]{0:T(1024)S(1)}, u32[]{:S(2)}) copy-start(f32[768]{0:T(1024)S(1)} %broadcast_multiply_fusion.9) | copy-start | bytes 9220
  374.8 41.0 %copy-start.44 = (f32[768]{0:T(1024)}, f32[768]{0:T(1024)S(1)}, u32[]{:S(2)}) copy-start(f32[768]{0:T(1024)S(1)} %add_rsqrt_fusion.1) | copy-start | bytes 9220
  396.2 13.6 %slice-start.2 = ((s8[4718592]{0:T(1024)(128)(4,1)}), s8[4194304]{0:T(1024)(128)(4,1)S(1)}, s32[]{:S(2)}) async-start(s8[4718592]{0:T(1024)(128)(4,1)} %bitcast.275), calls=%async_computation.27 | async-start | bytes 8388608
  419.4 14.9 %all-to-all-start.4 = ((bf16[768,2,384]{0,2,1:T(8,128)(2,1)}), bf16[768,2,384]{0,2,1:T(8,128)(2,1)S(1)}, u32[]{:S(2)}, u32[]{:S(2)}) async-start(bf16[768,2,384]{0,2,1:T(8,128)(2,1)} %bitcast.272), calls=%async_computation.4 | async-start | bytes 2359296 | tf_op jit(solution)/shard_map/all_to_all | solution.py:319
  423.2 751.5 %reduce-scatter.10.cloned.1.call-start = ((), (), s32[]{:S(2)}) async-start(), calls=%async_computation.19 | async-start | bytes 2506752 | tf_op jit(solution)/shard_map/reduce_scatter | solution.py:361
  427.1 749.3 %reduce-scatter.18.cloned.1.call-start = ((), (), s32[]{:S(2)}) async-start(), calls=%async_computation.23 | async-start | bytes 2506752
  721.5 14.0 %copy-start.24 = (bf16[768,768]{1,0:T(8,128)(2,1)S(1)}, bf16[768,768]{1,0:T(8,128)(2,1)}, u32[]{:S(2)}) copy-start(bf16[768,768]{1,0:T(8,128)(2,1)} %param.24) | copy-start | bytes 3538948
  738.5 439.5 %reduce-scatter.16.cloned.1.call-start = ((), (), s32[]{:S(2)}) async-start(), calls=%async_computation.22 | async-start | bytes 2506752
  773.6 406.2 %reduce-scatter.12.cloned.1.call-start = ((), (), s32[]{:S(2)}) async-start(), calls=%async_computation.20 | async-start | bytes 10027008 | tf_op jit(solution)/shard_map/reduce_scatter | solution.py:365
  784.3 405.1 %reduce-scatter.14.cloned.1.call-start = ((), (), s32[]{:S(2)}) async-start(), calls=%async_computation.21 | async-start | bytes 10027008 | tf_op jit(solution)/shard_map/reduce_scatter | solution.py:367
  802.9 74.3 %copy-start.16 = (bf16[768,768]{0,1:T(8,128)(2,1)S(1)}, bf16[768,768]{0,1:T(8,128)(2,1)}, u32[]{:S(2)}) copy-start(bf16[768,768]{0,1:T(8,128)(2,1)} %get-tuple-element.673) | copy-start | bytes 3538948
  802.9 80.7 %all-to-all-start.5 = ((bf16[2,768,768]{1,2,0:T(8,128)(2,1)}), bf16[2,768,768]{1,2,0:T(8,128)(2,1)S(1)}, u32[]{:S(2)}, u32[]{:S(2)}) async-start(bf16[2,768,768]{1,2,0:T(8,128)(2,1)} %copy.168), calls=%async_computation.5 | async-start | bytes 4718592 | tf_op jit(solution)/shard_map/all_to_all | solution.py:326
  806.8 439.8 %all-reduce.22.cloned.1.call-start = ((), (), s32[]{:S(2)}) async-start(), calls=%async_computation.24 | async-start | bytes 2703360 | tf_op jit(solution)/shard_map/psum | solution.py:373
  896.2 12.2 copy-start.49
  896.2 12.2 copy-start.51
  908.4 263.7 %copy-start.28 = (bf16[768,768]{0,1:T(8,128)(2,1)S(1)}, bf16[768,768]{0,1:T(8,128)(2,1)}, u32[]{:S(2)}) copy-start(bf16[768,768]{0,1:T(8,128)(2,1)} %copy-done.27) | copy-start | bytes 3538948
  908.4 263.7 %copy-start.57 = (bf16[768,768]{1,0:T(8,128)(2,1)S(1)}, bf16[768,768]{1,0:T(8,128)(2,1)}, u32[]{:S(2)}) copy-start(bf16[768,768]{1,0:T(8,128)(2,1)} %all-gather.9.cloned.1.call-done) | copy-start | bytes 3538948
  1174.7 16.6 %copy-start.13 = (f32[768,768]{0,1:T(8,128)S(1)}, f32[768,768]{0,1:T(8,128)}, u32[]{:S(2)}) copy-start(f32[768,768]{0,1:T(8,128)} %copy-done.11) | copy-start | bytes 7077892
  (151 other events, 763.9 us)
Sparse Core Ops, SparseCore 0:
  10.3 41.0 all-gather.10
  53.6 37.2 all-gather.8
  93.2 52.2 all-gather.6
  147.6 36.9 all-gather.12
  186.7 52.1 all-gather.14
  241.0 51.9 all-gather.16
  427.8 60.7 reduce-scatter.9
  738.7 64.5 reduce-scatter.17
  807.1 62.1 reduce-scatter.15
  873.8 158.2 reduce-scatter.11
  1036.2 153.1 reduce-scatter.13
  1193.3 53.2 all-reduce.21
where the time goes:
time: 1270 us; the launch traced here: 1260 us
  blocking collectives  420 us (33%)
  matrix products  301 us (24%)
  waiting for transfers between devices  225 us (18%)
  local copies, waits for them, and re-layouts  175 us (14%)
  other arithmetic  53.3 us (4%)
  loops' own time  45.1 us (4%)
  starting transfers between devices  24.5 us (2%)
  between operations  17.8 us (1%)
    unnamed x2, blocking collectives  310 us
    psum x1, blocking collectives, local(): totals = lax.psum(squares, ('dp', 'seq'))  67 us
    all_gather x1, waiting for transfers between devices, local(): lax.all_gather(query_weight, 'dp', axis=1, tiled=True)  50.5 us
    dot_general x18, matrix products, block_work(): jnp.einsum('qhc,khc->hqk', query_block, key_pair, preferred_element_type=...  49.7 us
    psum x1, waiting for transfers between devices, local(): lax.psum(shares[0].astype(jnp.bfloat16), 'seq').astype(jnp.float32)  44.9 us
    dot_general x9, matrix products, block_work(): jnp.einsum('hqk,qhc->khc', weights.astype(jnp.bfloat16), grad_block, pref...  42.1 us
    all_gather x1, waiting for transfers between devices, local(): lax.all_gather(value_weight, 'dp', axis=0, tiled=True)  38.2 us
    dot_general x9, matrix products, block_work(): jnp.einsum('qhc,khc->hqk', grad_block, value_pair, preferred_element_type...  33.5 us
  transfers between devices with their start and end apart: 18, of which 8 were waited for; matrix products, arithmetic and copies ran while one was open for 35% of the time, Pallas kernels for 0%

commit v1 on v0

v1 whole, which is shorter than its diff:
```python
import functools

import jax
import jax.numpy as jnp
from jax import lax
from jax.experimental import pallas as pl
from jax.experimental.pallas import tpu as pltpu
from jax.sharding import PartitionSpec as P

D = 768
HEADS = 12
HD = 64
PAIRS = HEADS // 2
LANES = 2 * HD
F32 = jnp.float32
BF = jnp.bfloat16
EPSILON = 1e-05
LN2 = 0.6931471805599453
QUERY_SCALE = HD**-0.5 / LN2
FORWARD_GROUPS = (1, 1, 2, 2)
VMEM_LIMIT = 58 * 1024 * 1024


def dot(left, right):
    return jnp.dot(left, right, preferred_element_type=F32)


def dot_rt(left, right):
    return lax.dot_general(left, right, (((1,), (1,)), ((), ())), preferred_element_type=F32)


def dot_lt(left, right):
    return lax.dot_general(left, right, (((0,), (0,)), ((), ())), preferred_element_type=F32)


def call(kernel, **kwargs):
    return pl.pallas_call(
        kernel, compiler_params=pltpu.CompilerParams(vmem_limit_bytes=VMEM_LIMIT), **kwargs
    )


def whole_block(shape):
    return pl.BlockSpec(shape, lambda step: (0,) * len(shape))


def pair_block(shape):
    return pl.BlockSpec((1,) + shape, lambda step: (step,) + (0,) * len(shape))


def weight_rows(pieces, columns=slice(None)):
    rows = [piece[0, :, :, columns].reshape(-1, piece[0, :, :, columns].shape[-1]) for piece in pieces]
    return rows[0] if len(rows) == 1 else jnp.concatenate(rows, axis=0)


def attention_forward_kernel(piece_count, own, other, own_entity, other_entity, *refs):
    pieces = refs[:piece_count]
    mixed, queries, keys, values, weights, totals, key_masked, value_ones, packed = refs[piece_count:]
    rows = own.shape[0]
    block = rows // 2
    lane = lax.broadcasted_iota(jnp.int32, (rows, LANES), 1)
    low = lane < HD
    at = 0
    for piece in pieces:
        part = piece[0].reshape(-1, D)
        packed[at : at + part.shape[0], :] = part
        at += part.shape[0]
    is_own = own_entity[...]
    is_other = other_entity[...]
    projected = dot(own[...], packed[...])
    entity_row = is_own > 0.5
    to_word = jnp.where(entity_row, projected[:, 256:384], projected[:, 0:128]) * QUERY_SCALE
    to_entity = jnp.where(entity_row, projected[:, 384:512], projected[:, 128:256]) * QUERY_SCALE
    queries[0, :, 0:LANES] = jnp.where(low, to_word, pltpu.roll(to_entity, HD, 1)).astype(BF)
    queries[0, :, LANES:] = jnp.where(low, pltpu.roll(to_word, HD, 1), to_entity).astype(BF)
    projected_other = dot(other[...], packed[:, 512:768])
    halves = (
        (projected[:, 512:640], projected[:, 640:768], is_own),
        (projected_other[:, 0:128], projected_other[:, 128:256], is_other),
    )
    for half, (key, value, entity) in enumerate(halves):
        at = pl.ds(half * rows, rows)
        keys[0, at, :] = key.astype(BF)
        values[0, at, :] = value.astype(BF)
        mask = jnp.where(low, 1.0 - entity, entity)
        turned = pltpu.roll(key, HD, 1)
        key_masked[at, 0:LANES] = (jnp.where(low, key, turned) * mask).astype(BF)
        key_masked[at, LANES:] = (jnp.where(low, turned, key) * mask).astype(BF)
        ones = jnp.ones_like(value)
        value_ones[at, 0:LANES] = jnp.where(low, value, ones).astype(BF)
        value_ones[at, LANES:] = jnp.where(low, ones, value).astype(BF)
    for index in range(rows // block):
        at = pl.ds(index * block, block)
        sums = []
        for head in range(2):
            columns = pl.ds(head * LANES, LANES)
            scores = dot_rt(queries[0, at, columns], key_masked[:, columns])
            highest = jnp.max(scores, axis=-1, keepdims=True)
            weight = jnp.exp2(scores - highest).astype(BF)
            weights[0, head, at, :] = weight
            sums.append(dot(weight, value_ones[:, columns]))
        upper = jnp.where(low[:block], sums[0], sums[1])
        total = pltpu.roll(jnp.where(low[:block], sums[1], sums[0]), HD, 1)
        mixed[at, :] = (upper / total).astype(BF)
        totals[0, at, :] = total


def piece_blocks(pieces):
    return [pair_block(piece.shape[1:]) for piece in pieces]


def attention_forward(own, other, own_entity, other_entity, pieces):
    count = pieces[0].shape[0]
    rows = own.shape[0]
    length = 2 * rows
    return call(
        functools.partial(attention_forward_kernel, len(pieces)),
        grid=(count,),
        in_specs=[whole_block((rows, D))] * 2 + [whole_block((rows, LANES))] * 2 + piece_blocks(pieces),
        out_specs=[
            pl.BlockSpec((rows, LANES), lambda step: (0, step)),
            pair_block((rows, 2 * LANES)),
            pair_block((length, LANES)),
            pair_block((length, LANES)),
            pair_block((2, rows, length)),
            pair_block((rows, LANES)),
        ],
        out_shape=[
            jax.ShapeDtypeStruct((rows, LANES * count), BF),
            jax.ShapeDtypeStruct((count, rows, 2 * LANES), BF),
            jax.ShapeDtypeStruct((count, length, LANES), BF),
            jax.ShapeDtypeStruct((count, length, LANES), BF),
            jax.ShapeDtypeStruct((count, 2, rows, length), BF),
            jax.ShapeDtypeStruct((count, rows, LANES), F32),
        ],
        scratch_shapes=[
            pltpu.VMEM((length, 2 * LANES), BF),
            pltpu.VMEM((length, 2 * LANES), BF),
            pltpu.VMEM((D, D), BF),
        ],
        name="attention_forward",
        cost_estimate=pl.CostEstimate(
            flops=count * 7_000_000_000, transcendentals=count * 2400000, bytes_accessed=count * 8_000_000
        ),
    )(own, other, own_entity, other_entity, *pieces)


def attention_backward_kernel(piece_count, first, own, other, own_entity, other_entity, *refs):
    pieces = refs[:piece_count]
    refs = refs[piece_count:]
    queries, keys, values, weights, totals, mixed, grad = refs[:7]
    refs = refs[7:]
    if not first:
        own_before, other_before = refs[:2]
        refs = refs[2:]
    near, far, own_grad, other_grad = refs[:4]
    key_masked, value_ones, grad_wide, query_grad, key_grad, value_grad, joined, packed = refs[4:]
    rows = own.shape[0]
    block = rows // 3
    lane = lax.broadcasted_iota(jnp.int32, (rows, LANES), 1)
    low = lane < HD
    at = 0
    for piece in pieces:
        part = piece[0].reshape(-1, D)
        packed[at : at + part.shape[0], :] = part
        at += part.shape[0]
    is_own = own_entity[...]
    is_other = other_entity[...]
    for half, entity in enumerate((is_own, is_other)):
        at = pl.ds(half * rows, rows)
        key = keys[0, at, :].astype(F32)
        turned = pltpu.roll(key, HD, 1)
        mask = jnp.where(low, 1.0 - entity, entity)
        key_masked[at, 0:LANES] = (jnp.where(low, key, turned) * mask).astype(BF)
        key_masked[at, LANES:] = (jnp.where(low, turned, key) * mask).astype(BF)
        value = values[0, at, :].astype(F32)
        ones = jnp.where(lane % HD < 2, 1.0, 0.0)
        value_ones[at, 0:LANES] = jnp.where(low, value, ones).astype(BF)
        value_ones[at, LANES:] = jnp.where(low, ones, value).astype(BF)
    scaled = grad[...].astype(F32) / totals[0]
    inner = scaled * mixed[...].astype(F32)

    def correction(inner_sum):
        upper = inner_sum.astype(BF).astype(F32)
        return jnp.where(
            lane % HD == 0, -upper, jnp.where(lane % HD == 1, upper - inner_sum, 0.0)
        )

    first_inner = jnp.sum(jnp.where(low, inner, 0.0), axis=-1, keepdims=True)
    second_inner = jnp.sum(jnp.where(low, 0.0, inner), axis=-1, keepdims=True)
    grad_wide[:, 0:LANES] = jnp.where(low, scaled, correction(first_inner)).astype(BF)
    grad_wide[:, LANES:] = jnp.where(low, correction(second_inner), scaled).astype(BF)
    for head in range(2):
        columns = pl.ds(head * LANES, LANES)
        for index in range(rows // block):
            at = pl.ds(index * block, block)
            grad_block = grad_wide[at, columns]
            weight = weights[0, head, at, :]
            score_grad = (weight.astype(F32) * dot_rt(grad_block, value_ones[:, columns])).astype(BF)
            query_grad[at, columns] = dot(score_grad, key_masked[:, columns]) * HD**-0.5
            query_turned = queries[0, at, columns].astype(F32).T.astype(BF)
            grad_turned = grad_block.astype(F32).T[head * HD : (head + 1) * HD].astype(BF)
            key_part = dot(query_turned, score_grad)
            value_part = dot(grad_turned, weight)
            key_at = pl.ds(head * LANES, LANES)
            value_at = pl.ds(head * HD, HD)
            if index == 0:
                key_grad[key_at, :] = key_part
                value_grad[value_at, :] = value_part
            else:
                key_grad[key_at, :] += key_part
                value_grad[value_at, :] += value_part
    query_a = query_grad[:, 0:LANES]
    query_b = query_grad[:, LANES:]
    word_grad = jnp.where(low, query_a, pltpu.roll(query_b, HD, 1))
    entity_grad = jnp.where(low, pltpu.roll(query_a, HD, 1), query_b)
    is_word = 1.0 - is_own
    joined[0:rows, 0:128] = (is_word * word_grad).astype(BF)
    joined[0:rows, 128:256] = (is_word * entity_grad).astype(BF)
    joined[0:rows, 256:384] = (is_own * word_grad).astype(BF)
    joined[0:rows, 384:512] = (is_own * entity_grad).astype(BF)
    key_back = key_grad[...].T
    value_back = value_grad[...].T
    for half, entity in enumerate((is_own, is_other)):
        at = slice(half * rows, half * rows + rows)
        key_a = key_back[at, 0:LANES]
        key_b = key_back[at, LANES:]
        key_word = jnp.where(low, key_a, pltpu.roll(key_b, HD, 1))
        key_entity = jnp.where(low, pltpu.roll(key_a, HD, 1), key_b)
        joined[at, 512:640] = (jnp.where(entity > 0.5, key_entity, key_word) * LN2).astype(BF)
        joined[at, 640:768] = value_back[at].astype(BF)
    here = dot_lt(own[...], joined[0:rows, :])
    there = dot_lt(other[...], joined[rows:, 512:768])
    for target, at in ((near, slice(0, D // 2)), (far, slice(D // 2, D))):
        target[0, :, 0:512] = here[at, 0:512].astype(BF)
        target[0, :, 512:768] = (here[at, 512:768] + there[at]).astype(BF)
    own_part = dot_rt(joined[0:rows, :], packed[...])
    other_part = dot_rt(joined[rows:, 512:768], packed[:, 512:768])
    step = pl.program_id(0)

    @pl.when(step == 0)
    def _():
        if first:
            own_grad[...] = own_part
            other_grad[...] = other_part
        else:
            own_grad[...] = own_before[...] + own_part
            other_grad[...] = other_before[...] + other_part

    @pl.when(step > 0)
    def _():
        own_grad[...] += own_part
        other_grad[...] += other_part


def attention_backward(own, other, own_entity, other_entity, pieces, saved, grad, before):
    count = pieces[0].shape[0]
    rows = own.shape[0]
    length = 2 * rows
    first = before is None
    column = pl.BlockSpec((rows, LANES), lambda step: (0, step))
    mixed, queries, keys, values, weights, totals = saved
    return call(
        functools.partial(attention_backward_kernel, len(pieces), first),
        grid=(count,),
        in_specs=[whole_block((rows, D))] * 2
        + [whole_block((rows, LANES))] * 2
        + piece_blocks(pieces)
        + [
            pair_block((rows, 2 * LANES)),
            pair_block((length, LANES)),
            pair_block((length, LANES)),
            pair_block((2, rows, length)),
            pair_block((rows, LANES)),
            column,
            column,
        ]
        + [whole_block((rows, D))] * (0 if first else 2),
        out_specs=[pair_block((D // 2, D))] * 2 + [whole_block((rows, D))] * 2,
        out_shape=[jax.ShapeDtypeStruct((count, D // 2, D), BF)] * 2
        + [jax.ShapeDtypeStruct((rows, D), F32)] * 2,
        scratch_shapes=[
            pltpu.VMEM((length, 2 * LANES), BF),
            pltpu.VMEM((length, 2 * LANES), BF),
            pltpu.VMEM((rows, 2 * LANES), BF),
            pltpu.VMEM((rows, 2 * LANES), F32),
            pltpu.VMEM((2 * LANES, length), F32),
            pltpu.VMEM((LANES, length), F32),
            pltpu.VMEM((length, D), BF),
            pltpu.VMEM((D, D), BF),
        ],
        name="attention_backward",
        cost_estimate=pl.CostEstimate(
            flops=count * 12_000_000_000, transcendentals=0, bytes_accessed=count * 12_000_000
        ),
    )(
        own, other, own_entity, other_entity, *pieces,
        queries, keys, values, weights, totals, mixed, grad, *(() if first else before),
    )


def error_function(value):
    value = jnp.clip(value, -3.7439211627767994, 3.7439211627767994)
    square = value * value
    upper = jnp.float32(0.00022905065861350646)
    for term in (
        0.0034082910107109506, 0.050955695062380861, 0.18520832239976145, 1.128379143519084,
    ):
        upper = upper * square + term
    lower = jnp.float32(-1.1791602954361697e-7)
    for term in (
        0.000023547966471313185, 0.0010179625278914885, 0.014070470171167667,
        0.11098505178285362, 0.49746925110067538, 1.0,
    ):
        lower = lower * square + term
    return value * upper / lower


def load_weights(copies):
    for copy in copies:
        copy.start()


def wait_all(copies):
    for copy in copies:
        copy.wait()


def feed_forward_kernel(
    group_count, piece_offsets, parts, position, vectors, tokens, cotangent, *refs
):
    piece_count = len(piece_offsets)
    mixed_groups = refs[:group_count]
    refs = refs[group_count:]
    mixing_pieces, up_pieces, down_pieces = (
        refs[k * piece_count : (k + 1) * piece_count] for k in range(3)
    )
    refs = refs[3 * piece_count :]
    (
        layer_out, near, far, hidden_low, slopes, normed_out, inverse_out, residual_grad, sums,
        mixing, up, down, active, total, hidden, low_grad, down_grad, in_sems, out_sems,
    ) = refs
    rows = tokens.shape[0]
    block = rows // 3
    me = position[0]

    def copies(source_pieces, target, index):
        made = []
        for k, offsets in enumerate(piece_offsets):
            for j, offset in enumerate(offsets):
                made.append((source_pieces[k].at[j], me ^ offset, len(made)))
        return made

    mixing_copies = [
        pltpu.make_async_copy(src, mixing.at[at], in_sems.at[0, n]) for src, at, n in copies(mixing_pieces, mixing, 0)
    ]
    up_copies = [
        pltpu.make_async_copy(src, up.at[:, at], in_sems.at[1, n]) for src, at, n in copies(up_pieces, up, 1)
    ]
    down_copies = [
        pltpu.make_async_copy(src, down.at[at], in_sems.at[2, n]) for src, at, n in copies(down_pieces, down, 2)
    ]
    load_weights(mixing_copies + up_copies + down_copies)
    chunk = parts // 4

    def vector(index):
        return vectors[index : index + 1, :]

    def add_sum(index, value, start):
        part = jnp.sum(value, axis=0, keepdims=True)
        if start:
            sums[index : index + 1, :] = part
        else:
            sums[index : index + 1, :] += part

    sums[6:8, :] = jnp.zeros((2, D), F32)
    wait_all(mixing_copies)
    for index in range(3):
        at = pl.ds(index * block, block)
        mixed = jnp.concatenate([group[at, :] for group in mixed_groups], axis=1)
        attended = dot(mixed, mixing[...].reshape(D, D)) + vector(0)
        stream = tokens[at, :].astype(F32) + attended
        add_sum(0, stream * stream, index == 0)
        add_sum(1, attended * attended, index == 0)
        center = stream - jnp.mean(stream, axis=-1, keepdims=True)
        inverse = lax.rsqrt(jnp.mean(center * center, axis=-1, keepdims=True) + EPSILON)
        normed = center * inverse
        normed_out[at, :] = normed
        inverse_out[at, :] = jnp.broadcast_to(inverse, (block, LANES))
        value = normed * vector(1) + vector(2)
        hidden[at, :] = value
        hidden_low[at, :] = value.astype(BF)
    wait_all(up_copies)
    wait_all(down_copies)
    for quarter in range(4):
        up_part = up[quarter].reshape(D, D)
        down_part = down[quarter * chunk : (quarter + 1) * chunk].reshape(D, D)
        for index in range(3):
            at = pl.ds(index * block, block)
            before = dot(hidden_low[at, :], up_part) + vector(6 + quarter)
            half = 0.5 * (1.0 + error_function(before * 0.7071067811865476))
            act = (before * half).astype(BF)
            active[quarter, at, :] = act
            slope = half + before * jnp.exp(-0.5 * before * before) * 0.3989422804014327
            slopes[at, quarter * D : (quarter + 1) * D] = slope.astype(BF)
            part = dot(act, down_part)
            if quarter == 0:
                total[at, :] = part
            else:
                total[at, :] += part
    for index in range(3):
        at = pl.ds(index * block, block)
        forward_out = total[at, :] + vector(3)
        add_sum(2, forward_out * forward_out, index == 0)
        value = hidden[at, :] + forward_out
        center = value - jnp.mean(value, axis=-1, keepdims=True)
        inverse = lax.rsqrt(jnp.mean(center * center, axis=-1, keepdims=True) + EPSILON)
        normed = center * inverse
        layer_out[at, :] = (normed * vector(4) + vector(5)).astype(BF)
        upstream = cotangent[at, :].astype(F32)
        scaled = upstream * vector(4)
        inner = (
            scaled
            - jnp.mean(scaled, axis=-1, keepdims=True)
            - normed * jnp.mean(scaled * normed, axis=-1, keepdims=True)
        ) * inverse
        residual_grad[at, :] = inner
        rounded = inner.astype(BF)
        low_grad[at, :] = rounded
        add_sum(3, upstream * normed, index == 0)
        add_sum(4, upstream, index == 0)
        add_sum(5, rounded.astype(F32), index == 0)
    for quarter in range(4):
        grad = dot_lt(active[quarter], low_grad[...])
        down_grad[quarter * chunk : (quarter + 1) * chunk] = grad.astype(BF).reshape(chunk, -1, D)
    store_relative(down_grad, near, far, me, piece_offsets, out_sems, lambda ref, at: ref.at[at])


def store_relative(source, near, far, me, piece_offsets, sems, pick):
    offsets = [offset for part in piece_offsets for offset in part]
    made = []
    for j, offset in enumerate(offsets):
        half = len(offsets) // 2
        target = near if j < half else far
        made.append(
            pltpu.make_async_copy(pick(source, me ^ offset), target.at[j % half], sems.at[j])
        )
    for copy in made:
        copy.start()
    for copy in made:
        copy.wait()


def feed_forward(position, vectors, tokens, cotangent, groups, weights, piece_offsets, parts):
    rows = tokens.shape[0]
    share = D // parts
    anywhere = pl.BlockSpec(memory_space=pl.ANY)
    vmem = pl.BlockSpec(memory_space=pltpu.VMEM)
    mixing_pieces, up_pieces, down_pieces = weights
    return call(
        functools.partial(feed_forward_kernel, len(groups), piece_offsets, parts),
        in_specs=[pl.BlockSpec(memory_space=pltpu.SMEM), vmem, vmem, vmem]
        + [vmem] * len(groups)
        + [anywhere] * (3 * len(piece_offsets)),
        out_specs=[vmem, anywhere, anywhere] + [vmem] * 6,
        out_shape=[
            jax.ShapeDtypeStruct((rows, D), BF),
            jax.ShapeDtypeStruct((parts // 2, 4 * share, D), BF),
            jax.ShapeDtypeStruct((parts // 2, 4 * share, D), BF),
            jax.ShapeDtypeStruct((rows, D), BF),
            jax.ShapeDtypeStruct((rows, 4 * D), BF),
            jax.ShapeDtypeStruct((rows, D), F32),
            jax.ShapeDtypeStruct((rows, LANES), F32),
            jax.ShapeDtypeStruct((rows, D), F32),
            jax.ShapeDtypeStruct((8, D), F32),
        ],
        scratch_shapes=[
            pltpu.VMEM((parts, share, D), BF),
            pltpu.VMEM((4, parts, share, D), BF),
            pltpu.VMEM((parts, 4 * share, D), BF),
            pltpu.VMEM((4, rows, D), BF),
            pltpu.VMEM((rows, D), F32),
            pltpu.VMEM((rows, D), F32),
            pltpu.VMEM((rows, D), BF),
            pltpu.VMEM((parts, 4 * share, D), BF),
            pltpu.SemaphoreType.DMA((3, parts)),
            pltpu.SemaphoreType.DMA((parts,)),
        ],
        name="feed_forward",
        cost_estimate=pl.CostEstimate(
            flops=12_000_000_000, transcendentals=4800000, bytes_accessed=40_000_000
        ),
    )(position, vectors, tokens, cotangent, *groups, *mixing_pieces, *up_pieces, *down_pieces)


def feed_back_kernel(
    group_count, piece_offsets, parts, position, vectors, hidden_low, slopes, normed, inverse,
    residual_grad, *refs
):
    piece_count = len(piece_offsets)
    mixed_groups = refs[:group_count]
    refs = refs[group_count:]
    mixing_pieces, up_pieces, down_pieces = (
        refs[k * piece_count : (k + 1) * piece_count] for k in range(3)
    )
    refs = refs[3 * piece_count :]
    up_near, up_far, mixing_near, mixing_far, stream_grad, sums = refs[:6]
    grad_groups = refs[6 : 6 + group_count]
    mixing, up, down, pre_grad, low_grad, back, up_grad, mixing_grad, in_sems, out_sems = refs[6 + group_count :]
    rows = hidden_low.shape[0]
    block = rows // 3
    me = position[0]
    chunk = parts // 4

    def copies(source_pieces):
        made = []
        for k, offsets in enumerate(piece_offsets):
            for j, offset in enumerate(offsets):
                made.append((source_pieces[k].at[j], me ^ offset, len(made)))
        return made

    down_copies = [
        pltpu.make_async_copy(src, down.at[at], in_sems.at[2, n]) for src, at, n in copies(down_pieces)
    ]
    up_copies = [
        pltpu.make_async_copy(src, up.at[:, at], in_sems.at[1, n]) for src, at, n in copies(up_pieces)
    ]
    mixing_copies = [
        pltpu.make_async_copy(src, mixing.at[at], in_sems.at[0, n]) for src, at, n in copies(mixing_pieces)
    ]
    load_weights(down_copies + up_copies + mixing_copies)

    def vector(index):
        return vectors[index : index + 1, :]

    def add_sum(index, value, start):
        part = jnp.sum(value, axis=0, keepdims=True)
        if start:
            sums[index : index + 1, :] = part
        else:
            sums[index : index + 1, :] += part

    sums[7:8, :] = jnp.zeros((1, D), F32)
    low_grad[...] = residual_grad[...].astype(BF)
    wait_all(down_copies)
    wait_all(up_copies)
    for quarter in range(4):
        up_part = up[quarter].reshape(D, D)
        down_part = down[quarter * chunk : (quarter + 1) * chunk].reshape(D, D)
        for index in range(3):
            at = pl.ds(index * block, block)
            slope = slopes[at, quarter * D : (quarter + 1) * D].astype(F32)
            part = (dot_rt(low_grad[at, :], down_part) * slope).astype(BF)
            pre_grad[at, :] = part
            add_sum(3 + quarter, part.astype(F32), index == 0)
            back_part = dot_rt(part, up_part)
            if quarter == 0:
                back[at, :] = back_part
            else:
                back[at, :] += back_part
        grad = dot_lt(hidden_low[...], pre_grad[...])
        up_grad[quarter] = grad.astype(BF).reshape(parts, -1, D)
    wait_all(mixing_copies)
    for index in range(3):
        at = pl.ds(index * block, block)
        hidden_grad = residual_grad[at, :] + back[at, :]
        norm = normed[at, :]
        scaled = hidden_grad * vector(1)
        inner = (
            scaled
            - jnp.mean(scaled, axis=-1, keepdims=True)
            - norm * jnp.mean(scaled * norm, axis=-1, keepdims=True)
        ) * inverse[at, 0:1]
        stream_grad[at, :] = inner
        rounded = inner.astype(BF)
        low_grad[at, :] = rounded
        add_sum(0, hidden_grad * norm, index == 0)
        add_sum(1, hidden_grad, index == 0)
        add_sum(2, rounded.astype(F32), index == 0)
        mixed_grad = dot_rt(rounded, mixing[...].reshape(D, D)).astype(BF)
        start = 0
        for group in grad_groups:
            width = group.shape[1]
            group[at, :] = mixed_grad[:, start : start + width]
            start += width
    start = 0
    for group in mixed_groups:
        width = group.shape[1]
        back[start : start + width, :] = dot_lt(group[...], low_grad[...])
        start += width
    mixing_grad[...] = back[...].astype(BF).reshape(parts, -1, D)
    store_relative(up_grad, up_near, up_far, me, piece_offsets, out_sems.at[0], lambda ref, at: ref.at[:, at])
    store_relative(mixing_grad, mixing_near, mixing_far, me, piece_offsets, out_sems.at[1], lambda ref, at: ref.at[at])


def feed_back(position, vectors, saved, groups, weights, piece_offsets, parts):
    hidden_low, slopes, normed, inverse, residual_grad = saved
    rows = hidden_low.shape[0]
    share = D // parts
    half = parts // 2
    anywhere = pl.BlockSpec(memory_space=pl.ANY)
    vmem = pl.BlockSpec(memory_space=pltpu.VMEM)
    mixing_pieces, up_pieces, down_pieces = weights
    return call(
        functools.partial(feed_back_kernel, len(groups), piece_offsets, parts),
        in_specs=[pl.BlockSpec(memory_space=pltpu.SMEM)]
        + [vmem] * (6 + len(groups))
        + [anywhere] * (3 * len(piece_offsets)),
        out_specs=[anywhere] * 4 + [vmem] * (2 + len(groups)),
        out_shape=[jax.ShapeDtypeStruct((half, 4, share, D), BF)] * 2
        + [jax.ShapeDtypeStruct((half, share, D), BF)] * 2
        + [jax.ShapeDtypeStruct((rows, D), F32), jax.ShapeDtypeStruct((8, D), F32)]
        + [jax.ShapeDtypeStruct(group.shape, BF) for group in groups],
        scratch_shapes=[
            pltpu.VMEM((parts, share, D), BF),
            pltpu.VMEM((4, parts, share, D), BF),
            pltpu.VMEM((parts, 4 * share, D), BF),
            pltpu.VMEM((rows, D), BF),
            pltpu.VMEM((rows, D), BF),
            pltpu.VMEM((rows, D), F32),
            pltpu.VMEM((4, parts, share, D), BF),
            pltpu.VMEM((parts, share, D), BF),
            pltpu.SemaphoreType.DMA((3, parts)),
            pltpu.SemaphoreType.DMA((2, parts)),
        ],
        name="feed_back",
        cost_estimate=pl.CostEstimate(
            flops=13_000_000_000, transcendentals=0, bytes_accessed=40_000_000
        ),
    )(position, vectors, hidden_low, slopes, normed, inverse, residual_grad, *groups,
      *mixing_pieces, *up_pieces, *down_pieces)


def swap(value, bit, axis="dp"):
    size = lax.axis_size(axis)
    return lax.ppermute(value, axis, [(index, index ^ bit) for index in range(size)])


def relative_offsets(size):
    offsets = [0]
    bit = size // 2
    while bit:
        offsets += [offset ^ bit for offset in offsets]
        bit //= 2
    return offsets


def gather_pieces(shard, axis):
    size = lax.axis_size("dp")
    held = jnp.expand_dims(shard, axis)
    bit = size // 2
    while bit > 2:
        held = jnp.concatenate([held, swap(held, bit)], axis=axis)
        bit //= 2
    beside = swap(held, 2)
    return [held, beside, swap(held, 1), swap(beside, 1)]


def scatter_sum(near, far, axis):
    kept, received = near, swap(far, 1)
    bit = 2
    while bit < lax.axis_size("dp"):
        half = kept.shape[axis] // 2
        first = lax.slice_in_dim(kept, 0, half, axis=axis) + lax.slice_in_dim(received, 0, half, axis=axis)
        second = lax.slice_in_dim(kept, half, 2 * half, axis=axis) + lax.slice_in_dim(received, half, 2 * half, axis=axis)
        kept, received = first, swap(second, bit)
        bit *= 2
    mine = kept + received
    mine = lax.squeeze(mine, (axis,))
    return mine.astype(F32) + swap(mine, 1, "seq").astype(F32)


def sum_everywhere(value, axes):
    for axis in axes:
        bit = 1
        while bit < lax.axis_size(axis):
            value = value + swap(value, bit, axis)
            bit *= 2
    return value


def local(
    tokens,
    entity_flags,
    query_weight,
    key_weight,
    value_weight,
    mixing_weight,
    mixing_bias,
    first_gain,
    first_bias,
    up_weight,
    up_bias,
    down_weight,
    down_bias,
    second_gain,
    second_bias,
    cotangent,
):
    parts = lax.axis_size("dp")
    me = lax.axis_index("dp")
    share = D // parts
    rows = tokens.shape[0]
    by_swaps = share % 16 == 0 and parts & (parts - 1) == 0 and parts > 4

    six = jnp.concatenate([query_weight, key_weight[None], value_weight[None]], axis=0)
    pairs = jnp.transpose(six.reshape(6, share, PAIRS, LANES), (2, 1, 0, 3)).reshape(PAIRS, share, D)
    up_shard = jnp.transpose(up_weight.reshape(share, 4, D), (1, 0, 2))

    offsets = relative_offsets(parts) if by_swaps else list(range(parts))
    order = me ^ jnp.array(offsets, jnp.int32) if by_swaps else jnp.array(offsets, jnp.int32)
    column_of = (order[:, None] * share + jnp.arange(share, dtype=jnp.int32)[None, :]).reshape(D)
    choose = (lax.broadcasted_iota(jnp.int32, (D, D), 0) == column_of[None, :]).astype(BF)
    own = dot(tokens, choose).astype(BF)
    other = swap(own, 1, "seq")
    entity = entity_flags.astype(F32)
    own_entity = jnp.broadcast_to(entity[:, None], (rows, LANES))
    other_entity = jnp.broadcast_to(swap(entity, 1, "seq")[:, None], (rows, LANES))

    blank = jnp.zeros((D,), BF)
    vectors = jnp.stack(
        [
            lax.dynamic_update_slice(blank, vector, (me * share,))
            for vector in (mixing_bias, first_gain, first_bias, down_bias, second_gain, second_bias)
        ]
    )
    up_vector = lax.dynamic_update_slice(jnp.zeros((4 * D,), BF), up_bias, (me * 4 * share,)).reshape(4, D)
    vectors = jnp.concatenate([vectors, up_vector, jnp.zeros((6, D), BF)], axis=0)

    groups = []
    start = 0
    if by_swaps:
        for count in FORWARD_GROUPS:
            groups.append(gather_pieces(pairs[start : start + count], 1))
            start += count
        middle = (
            gather_pieces(mixing_weight, 0),
            gather_pieces(up_shard, 0),
            gather_pieces(down_weight, 0),
        )
        vectors = sum_everywhere(vectors, ("dp",))
        middle_offsets = [offsets[k * parts // 4 : (k + 1) * parts // 4] for k in range(4)]
        position, middle_parts = me, parts
    else:
        for count in FORWARD_GROUPS:
            gathered = lax.all_gather(pairs[start : start + count], "dp", axis=1, tiled=True)
            groups.append([gathered.reshape(count, 1, D, D)])
            start += count
        joined = [
            lax.all_gather(weight, "dp", axis=0, tiled=True)
            for weight in (mixing_weight, up_weight, down_weight)
        ]
        vectors = lax.psum(vectors, "dp")
        middle_parts = 4
        middle = (
            [joined[0].reshape(4, D // 4, D)],
            [jnp.transpose(joined[1].reshape(4, D // 4, 4, D), (0, 2, 1, 3))],
            [joined[2].reshape(4, D, D)],
        )
        middle_offsets = [[0, 1, 2, 3]]
        position = jnp.int32(0)
    vectors = vectors.astype(F32)
    position = position.astype(jnp.int32).reshape(1)

    saved = [attention_forward(own, other, own_entity, other_entity, pieces) for pieces in groups]
    mixed = [item[0] for item in saved]
    (
        layer_out, down_near, down_far, hidden_low, slopes, normed, inverse, residual_grad, sums_one,
    ) = feed_forward(position, vectors, tokens, cotangent, mixed, middle, middle_offsets, middle_parts)
    up_near, up_far, mixing_near, mixing_far, stream_grad, sums_two, *mixed_grads = feed_back(
        position, vectors, (hidden_low, slopes, normed, inverse, residual_grad), mixed, middle,
        middle_offsets, middle_parts,
    )

    before = None
    parts_of = [None] * len(groups)
    for index in reversed(range(len(groups))):
        near, far, *before = attention_backward(
            own, other, own_entity, other_entity, groups[index], saved[index], mixed_grads[index], before
        )
        parts_of[index] = (near, far)
    own_grad, other_grad = before
    attended = own_grad + swap(other_grad.astype(BF), 1, "seq").astype(F32)
    upper = attended.astype(BF)
    lower = (attended - upper.astype(F32)).astype(BF)
    tokens_grad = (stream_grad + dot_rt(upper, choose) + dot_rt(lower, choose)).astype(BF)

    sums = jnp.concatenate([sums_one, sums_two], axis=0)
    if by_swaps:
        down_sum = scatter_sum(down_near, down_far, 0)
        up_sum = scatter_sum(up_near, up_far, 0)
        mixing_sum = scatter_sum(mixing_near, mixing_far, 0)
        pair_sums = []
        for near, far in parts_of:
            shape = (near.shape[0], parts // 2, share, D)
            pair_sums.append(scatter_sum(near.reshape(shape), far.reshape(shape), 1))
        pair_sum = jnp.concatenate(pair_sums, axis=0)
        sums = sum_everywhere(sums, ("dp", "seq"))
    else:

        def reduced(near, far, axis):
            value = jnp.concatenate([near, far], axis=axis)
            piece = lax.psum_scatter(value.reshape(value.shape), "dp", scatter_dimension=axis, tiled=True)
            return lax.psum(piece, "seq").astype(F32)

        down_sum = reduced(down_near.reshape(-1, D), down_far.reshape(-1, D), 0)
        up_all = jnp.concatenate([up_near, up_far], axis=0)
        up_sum = reduced(
            *jnp.split(jnp.transpose(up_all, (1, 0, 2, 3)).reshape(4, D, D), 2, axis=1), 1
        )
        mixing_sum = reduced(mixing_near.reshape(-1, D), mixing_far.reshape(-1, D), 0)
        pair_sum = jnp.concatenate([reduced(near, far, 1) for near, far in parts_of], axis=0)
        sums = lax.psum(sums, ("dp", "seq"))

    six_sum = jnp.transpose(pair_sum.reshape(PAIRS, share, 6, LANES), (2, 1, 0, 3)).reshape(6, share, D)
    up_out = jnp.transpose(up_sum, (1, 0, 2)).reshape(share, 4 * D)

    def shard(row, width=1):
        return lax.dynamic_slice(sums[row : row + width].reshape(-1), (me * share * width,), (share * width,))

    token_count = rows * parts * lax.axis_size("seq")
    stream_rms = jnp.sqrt(jnp.sum(sums[0:3], axis=1) / (token_count * D))
    return (
        layer_out,
        tokens_grad,
        six_sum[0:4],
        six_sum[4],
        six_sum[5],
        mixing_sum,
        shard(10),
        shard(8),
        shard(9),
        up_out,
        shard(11, 4),
        down_sum,
        shard(5),
        shard(3),
        shard(4),
        stream_rms,
    )


def solution(mesh):
    rows = P(("dp", "seq"), None)
    vector = P("dp")
    matrix = P("dp", None)
    stacked = P(None, "dp", None)
    in_specs = (
        rows, P(("dp", "seq")), stacked, matrix, matrix, matrix, vector, vector, vector, matrix,
        vector, matrix, vector, vector, vector, rows,
    )
    out_specs = (
        rows, rows, stacked, matrix, matrix, matrix, vector, vector, vector, matrix, vector,
        matrix, vector, vector, vector, P(),
    )
    return jax.shard_map(local, mesh=mesh, in_specs=in_specs, out_specs=out_specs, check_vma=False)
```

time: 1270 us -> 609 us (0.48)
  blocking collectives: 420 us -> 0 us
  matrix products: 301 us -> 4.67 us
  Pallas kernels: 0 us -> 199 us
  local copies, waits for them, and re-layouts: 175 us -> 31.8 us
  waiting for transfers between devices: 225 us -> 273 us
  loops' own time: 45.1 us -> 0 us
  starting transfers between devices: 24.5 us -> 68.4 us
  other arithmetic: 53.3 us -> 19.4 us
  between operations: 17.8 us -> 1.91 us
    unnamed x2 -> x0, blocking collectives: 310 us -> none
    dot_general x81 -> x3, matrix products: 301 us -> 4.67 us  [the longest x2 2.5 us: dot_rt(): lax.dot_general(left, right, (((1,), (1,)), ((), ())), preferred_element_...]
    ppermute x0 -> x82, waiting for transfers between devices: none -> 273 us  [swap(): lax.ppermute(value, axis, [(index, index ^ bit) for index in range(size)])]
    pallas_call x0 -> x10, Pallas kernels: none -> 199 us  [the longest x4 79.1 us: attention_backward(): call(functools.partial(attention_backward_kernel, len(pieces), first), gr...]
    all_gather x6 -> x0, waiting for transfers between devices: 121 us -> none  [the longest x1 50.5 us: local(): lax.all_gather(query_weight, 'dp', axis=1, tiled=True)]
    psum x2 -> x0, blocking collectives: 72.2 us -> none  [the longest x1 67 us: local(): totals = lax.psum(squares, ('dp', 'seq'))]
    ppermute x0 -> x82, starting transfers between devices: none -> 68.4 us  [swap(): lax.ppermute(value, axis, [(index, index ^ bit) for index in range(size)])]
    all_to_all x6 -> x0, waiting for transfers between devices: 47.6 us -> none  [the longest x1 21.3 us: local(): lax.all_to_all(keys_masked, 'seq', split_axis=1, concat_axis=0, tiled=True)]
  transfers between devices with their start and end apart: 18 -> 82, of which waited for: 8 -> 33; matrix products, arithmetic and copies ran while one was open for 35% -> 7% of each run, Pallas kernels for 0% -> 23%
where the time goes in v1:
time: 609 us; the launch traced here: 598 us
  waiting for transfers between devices  273 us (45%)
  Pallas kernels  199 us (33%)
  starting transfers between devices  68.4 us (11%)
  local copies, waits for them, and re-layouts  31.8 us (5%)
  other arithmetic  19.4 us (3%)
    ppermute x82, waiting for transfers between devices, swap(): lax.ppermute(value, axis, [(index, index ^ bit) for index in range(size)])  273 us
    pallas_call x4, Pallas kernels, attention_backward(): call(functools.partial(attention_backward_kernel, len(pieces), first), gr...  79.1 us
    ppermute x82, starting transfers between devices, swap(): lax.ppermute(value, axis, [(index, index ^ bit) for index in range(size)])  68.4 us
    pallas_call x4, Pallas kernels, attention_forward(): call(functools.partial(attention_forward_kernel, len(pieces)), grid=(coun...  57.9 us
    pallas_call x1, Pallas kernels, feed_forward(): call(functools.partial(feed_forward_kernel, len(groups), piece_offsets, p...  34.8 us
    pallas_call x1, Pallas kernels, feed_back(): call(functools.partial(feed_back_kernel, len(groups), piece_offsets, part...  27.2 us
  transfers between devices with their start and end apart: 82, of which 33 were waited for; matrix products, arithmetic and copies ran while one was open for 7% of the time, Pallas kernels for 23%

profile of v1, /device:TPU:0, one launch (start us, length us, event | category | flops | bytes accessed | tf_op | source)
XLA Modules:
  0.0 598.3 jit_solution(1801539714594242772)
XLA Ops:
  28.1 6.8 %collective-permute-done.2 = bf16[16,768]{1,0:T(8,128)(2,1)S(1)} collective-permute-done((bf16[16,768]{1,0:T(8,128)(2,1)S(1)}, bf16[16,768]{1,0:T(8,128)(2,1)S(1)}, u32[]{:S(2)}, u32[]{:S(2)}) %collective-permute-start.2) | collective-permute-done | bytes 24608 | tf_op jit(solution)/shard_map/ppermute | solution.py:635
  41.1 23.7 %collective-permute-done.3 = bf16[16,768]{1,0:T(8,128)(2,1)S(1)} collective-permute-done((bf16[16,768]{1,0:T(8,128)(2,1)S(1)}, bf16[16,768]{1,0:T(8,128)(2,1)S(1)}, u32[]{:S(2)}, u32[]{:S(2)}) %collective-permute-start.3) | collective-permute-done | bytes 24608 | tf_op jit(solution)/shard_map/ppermute | solution.py:635
  69.3 7.6 %collective-permute-done.12 = bf16[1,2,48,768]{3,2,1,0:T(8,128)(2,1)S(1)} collective-permute-done((bf16[1,2,48,768]{3,2,1,0:T(8,128)(2,1)S(1)}, bf16[1,2,48,768]{3,2,1,0:T(8,128)(2,1)S(1)}, u32[]{:S(2)}, u32[]{:S(2)}) %collective-permute-start.12) | collective-permute-done | bytes 147488 | tf_op jit(solution)/shard_map/ppermute | solution.py:635
  79.1 7.3 %collective-permute-done.7 = bf16[1,2,48,768]{3,2,1,0:T(8,128)(2,1)S(1)} collective-permute-done((bf16[1,2,48,768]{3,2,1,0:T(8,128)(2,1)S(1)}, bf16[1,2,48,768]{3,2,1,0:T(8,128)(2,1)S(1)}, u32[]{:S(2)}, u32[]{:S(2)}) %collective-permute-start.7) | collective-permute-done | bytes 147488 | tf_op jit(solution)/shard_map/ppermute | solution.py:635
  88.5 16.8 %collective-permute-done.17 = bf16[2,2,48,768]{3,2,1,0:T(8,128)(2,1)S(1)} collective-permute-done((bf16[2,2,48,768]{3,2,1,0:T(8,128)(2,1)S(1)}, bf16[2,2,48,768]{3,2,1,0:T(8,128)(2,1)S(1)}, u32[]{:S(2)}, u32[]{:S(2)}) %collective-permute-start.17) | collective-permute-done | bytes 294944 | tf_op jit(solution)/shard_map/ppermute | solution.py:635
  107.8 8.1 %collective-permute-done.37 = bf16[2,192,768]{2,1,0:T(8,128)(2,1)S(1)} collective-permute-done((bf16[2,192,768]{2,1,0:T(8,128)(2,1)S(1)}, bf16[2,192,768]{2,1,0:T(8,128)(2,1)S(1)}, u32[]{:S(2)}, u32[]{:S(2)}) %collective-permute-start.37) | collective-permute-done | bytes 589856 | tf_op jit(solution)/shard_map/ppermute | solution.py:635
  124.2 9.3 %attention_forward.5 = (bf16[768,128]{1,0:T(8,128)(2,1)}, bf16[1,768,256]{2,1,0:T(8,128)(2,1)}, bf16[1,1536,128]{2,1,0:T(8,128)(2,1)}, bf16[1,1536,128]{2,1,0:T(...) custom-call(bf16[768,768]{1,0:T(8,128)(2,1)} %fusion.6.own, bf16[768,768]{1,0:T(8,128)(2,1)} %copy-done.28, ...), custom_call_target="tpu_custom_call" | custom-call | flops 7000000000 | bytes 8000000 | tf_op jit(solution)/shard_map/attention_forward/pallas_call | solution.py:115
  135.5 6.6 %collective-permute-done.23.refs_1_ = bf16[2,4,48,768]{3,2,1,0:T(8,128)(2,1)} collective-permute-done((bf16[2,4,48,768]{3,2,1,0:T(8,128)(2,1)S(1)}, bf16[2,4,48,768]{3,2,1,0:T(8,128)(2,1)}, u32[]{:S(2)}, u32[]{:S(2)}) %collective-permute-start.23) | collective-permute-done | bytes 589856 | tf_op jit(solution)/shard_map/ppermute | solution.py:635
  142.2 19.1 %attention_forward.4 = (bf16[768,128]{1,0:T(8,128)(2,1)}, bf16[1,768,256]{2,1,0:T(8,128)(2,1)}, bf16[1,1536,128]{2,1,0:T(8,128)(2,1)}, bf16[1,1536,128]{2,1,0:T(...) custom-call(bf16[768,768]{1,0:T(8,128)(2,1)} %fusion.6.own, bf16[768,768]{1,0:T(8,128)(2,1)} %copy-done.28, ...), custom_call_target="tpu_custom_call" | custom-call | flops 7000000000 | bytes 8000000 | tf_op jit(solution)/shard_map/attention_forward/pallas_call | solution.py:115
  164.2 14.3 %attention_forward.7 = (bf16[768,256]{1,0:T(8,128)(2,1)}, bf16[2,768,256]{2,1,0:T(8,128)(2,1)}, bf16[2,1536,128]{2,1,0:T(8,128)(2,1)}, bf16[2,1536,128]{2,1,0:T(...) custom-call(bf16[768,768]{1,0:T(8,128)(2,1)} %fusion.6.own, bf16[768,768]{1,0:T(8,128)(2,1)} %copy-done.28, ...), custom_call_target="tpu_custom_call" | custom-call | flops 14000000000 | bytes 16000000 | tf_op jit(solution)/shard_map/attention_forward/pallas_call | solution.py:115
  179.4 11.3 %collective-permute-done.38.refs_13_ = bf16[4,192,768]{2,1,0:T(8,128)(2,1)S(1)} collective-permute-done((bf16[4,192,768]{2,1,0:T(8,128)(2,1)S(1)}, bf16[4,192,768]{2,1,0:T(8,128)(2,1)S(1)}, u32[]{:S(2)}, u32[]{:S(2)}) %collective-permute-start.38) | collective-permute-done | bytes 1179680 | tf_op jit(solution)/shard_map/ppermute | solution.py:635
  190.7 24.6 %collective-permute-done.33.refs_9_ = bf16[4,4,48,768]{3,2,1,0:T(8,128)(2,1)S(1)} collective-permute-done((bf16[4,4,48,768]{3,2,1,0:T(8,128)(2,1)S(1)}, bf16[4,4,48,768]{3,2,1,0:T(8,128)(2,1)S(1)}, u32[]{:S(2)}, u32[]{:S(2)}) %collective-permute-start.33) | collective-permute-done | bytes 1179680 | tf_op jit(solution)/shard_map/ppermute | solution.py:635
  215.3 15.2 %attention_forward.6 = (bf16[768,256]{1,0:T(8,128)(2,1)}, bf16[2,768,256]{2,1,0:T(8,128)(2,1)}, bf16[2,1536,128]{2,1,0:T(8,128)(2,1)}, bf16[2,1536,128]{2,1,0:T(...) custom-call(bf16[768,768]{1,0:T(8,128)(2,1)} %fusion.6.own, bf16[768,768]{1,0:T(8,128)(2,1)} %copy-done.28, ...), custom_call_target="tpu_custom_call" | custom-call | flops 14000000000 | bytes 16000000 | tf_op jit(solution)/shard_map/attention_forward/pallas_call | solution.py:115
  231.6 34.8 %feed_forward.1 = (bf16[768,768]{1,0:T(8,128)(2,1)}, bf16[8,192,768]{2,1,0:T(8,128)(2,1)}, bf16[8,192,768]{2,1,0:T(8,128)(2,1)}, bf16[768,768]{1,0:T(8,128)(2,1)...) custom-call(s32[1]{0:T(128)} %bitcast.position, ...), custom_call_target="tpu_custom_call" | custom-call | flops 12000000000 | bytes 40000000 | tf_op jit(solution)/shard_map/feed_forward/pallas_call | solution.py:459
  267.2 27.2 %feed_back.1 = (bf16[8,4,48,768]{3,2,1,0:T(8,128)(2,1)}, bf16[8,4,48,768]{3,2,1,0:T(8,128)(2,1)}, bf16[8,48,768]{2,1,0:T(8,128)(2,1)}, bf16[8,48,768]{2,1,0:T(8,...) custom-call(s32[1]{0:T(128)} %bitcast.position, ...), custom_call_target="tpu_custom_call" | custom-call | flops 12999999488 | bytes 40000000 | tf_op jit(solution)/shard_map/feed_back/pallas_call | solution.py:603
  295.2 23.4 %attention_backward.4 = (bf16[2,384,768]{2,1,0:T(8,128)(2,1)}, bf16[2,384,768]{2,1,0:T(8,128)(2,1)}, f32[768,768]{1,0:T(8,128)}, f32[768,768]{1,0:T(8,128)}) custom-call(bf16[768,768]{1,0:T(8,128)(2,1)} %fusion.6.own, bf16[768,768]{1,0:T(8,128)(2,1)} %copy-done.28, f32[768,128]{1,0:T(8,128)} %broadcast_in_dim.49.own_entity, ...), custom_call_target="tpu_custom_call" | custom-call | flops 24000000000 | bytes 24000000 | tf_op jit(solution)/shard_map/attention_backward/pallas_call | solution.py:262
  318.6 25.6 %attention_backward.5 = (bf16[2,384,768]{2,1,0:T(8,128)(2,1)}, bf16[2,384,768]{2,1,0:T(8,128)(2,1)}, f32[768,768]{1,0:T(8,128)}, f32[768,768]{1,0:T(8,128)}) custom-call(bf16[768,768]{1,0:T(8,128)(2,1)} %fusion.6.own, bf16[768,768]{1,0:T(8,128)(2,1)} %copy-done.28, f32[768,128]{1,0:T(8,128)} %broadcast_in_dim.49.own_entity, ...), custom_call_target="tpu_custom_call" | custom-call | flops 24000000000 | bytes 24000000 | tf_op jit(solution)/shard_map/attention_backward/pallas_call | solution.py:262
  346.1 14.9 %attention_backward.6 = (bf16[1,384,768]{2,1,0:T(8,128)(2,1)}, bf16[1,384,768]{2,1,0:T(8,128)(2,1)}, f32[768,768]{1,0:T(8,128)}, f32[768,768]{1,0:T(8,128)}) custom-call(bf16[768,768]{1,0:T(8,128)(2,1)} %fusion.6.own, bf16[768,768]{1,0:T(8,128)(2,1)} %copy-done.28, f32[768,128]{1,0:T(8,128)} %broadcast_in_dim.49.own_entity, ...), custom_call_target="tpu_custom_call" | custom-call | flops 12000000000 | bytes 12000000 | tf_op jit(solution)/shard_map/attention_backward/pallas_call | solution.py:262
  361.3 15.2 %attention_backward.7 = (bf16[1,384,768]{2,1,0:T(8,128)(2,1)}, bf16[1,384,768]{2,1,0:T(8,128)(2,1)}, f32[768,768]{1,0:T(8,128)}, f32[768,768]{1,0:T(8,128)}) custom-call(bf16[768,768]{1,0:T(8,128)(2,1)} %fusion.6.own, bf16[768,768]{1,0:T(8,128)(2,1)} %copy-done.28, f32[768,128]{1,0:T(8,128)} %broadcast_in_dim.49.own_entity, ...), custom_call_target="tpu_custom_call" | custom-call | flops 12000000000 | bytes 12000000 | tf_op jit(solution)/shard_map/attention_backward/pallas_call | solution.py:262
  401.8 5.4 collective-permute-done.43
  407.5 6.0 %collective-permute-done.48 = bf16[1,4,48,768]{3,2,1,0:T(8,128)(2,1)S(1)} collective-permute-done((bf16[1,4,48,768]{3,2,1,0:T(8,128)(2,1)S(1)}, bf16[1,4,48,768]{3,2,1,0:T(8,128)(2,1)S(1)}, u32[]{:S(2)}, u32[]{:S(2)}) %collective-permute-start.48) | collective-permute-done | bytes 294944 | tf_op jit(solution)/shard_map/ppermute | solution.py:635
  413.6 5.0 collective-permute-done.63
  443.0 4.9 collective-permute-done.50
  474.5 10.0 %collective-permute-done.58 = bf16[2,4,48,768]{3,2,0,1:T(8,128)(2,1)S(1)} collective-permute-done((bf16[2,4,48,768]{3,2,0,1:T(8,128)(2,1)S(1)}, bf16[2,4,48,768]{3,2,0,1:T(8,128)(2,1)S(1)}, u32[]{:S(2)}, u32[]{:S(2)}) %collective-permute-start.58) | collective-permute-done | bytes 589856 | tf_op jit(solution)/shard_map/ppermute | solution.py:635
  486.0 10.7 %collective-permute-done.53 = bf16[2,4,48,768]{3,2,0,1:T(8,128)(2,1)S(1)} collective-permute-done((bf16[2,4,48,768]{3,2,0,1:T(8,128)(2,1)S(1)}, bf16[2,4,48,768]{3,2,0,1:T(8,128)(2,1)S(1)}, u32[]{:S(2)}, u32[]{:S(2)}) %collective-permute-start.53) | collective-permute-done | bytes 589856 | tf_op jit(solution)/shard_map/ppermute | solution.py:635
  502.2 6.4 %collective-permute-done.54 = bf16[2,2,48,768]{3,2,0,1:T(8,128)(2,1)S(1)} collective-permute-done((bf16[2,2,48,768]{3,2,0,1:T(8,128)(2,1)S(1)}, bf16[2,2,48,768]{3,2,0,1:T(8,128)(2,1)S(1)}, u32[]{:S(2)}, u32[]{:S(2)}) %collective-permute-start.54) | collective-permute-done | bytes 294944 | tf_op jit(solution)/shard_map/ppermute | solution.py:635
  509.5 7.5 %collective-permute-done.55 = bf16[2,1,48,768]{3,2,0,1:T(8,128)(2,1)S(1)} collective-permute-done((bf16[2,1,48,768]{3,2,0,1:T(8,128)(2,1)S(1)}, bf16[2,1,48,768]{3,2,0,1:T(8,128)(2,1)S(1)}, u32[]{:S(2)}, u32[]{:S(2)}) %collective-permute-start.55) | collective-permute-done | bytes 147488 | tf_op jit(solution)/shard_map/ppermute | solution.py:635
  517.6 11.2 %collective-permute-done.73 = bf16[4,4,48,768]{3,2,1,0:T(8,128)(2,1)S(1)} collective-permute-done((bf16[4,4,48,768]{3,2,1,0:T(8,128)(2,1)S(1)}, bf16[4,4,48,768]{3,2,1,0:T(8,128)(2,1)S(1)}, u32[]{:S(2)}, u32[]{:S(2)}) %collective-permute-start.73) | collective-permute-done | bytes 1179680 | tf_op jit(solution)/shard_map/ppermute | solution.py:635
  529.7 22.5 %collective-permute-done.78 = bf16[4,192,768]{2,1,0:T(8,128)(2,1)S(1)} collective-permute-done((bf16[4,192,768]{2,1,0:T(8,128)(2,1)S(1)}, bf16[4,192,768]{2,1,0:T(8,128)(2,1)S(1)}, u32[]{:S(2)}, u32[]{:S(2)}) %collective-permute-start.78) | collective-permute-done | bytes 1179680 | tf_op jit(solution)/shard_map/ppermute | solution.py:635
  556.8 16.5 %collective-permute-done.79 = bf16[2,192,768]{2,1,0:T(8,128)(2,1)} collective-permute-done((bf16[2,192,768]{2,1,0:T(8,128)(2,1)}, bf16[2,192,768]{2,1,0:T(8,128)(2,1)}, u32[]{:S(2)}, u32[]{:S(2)}) %collective-permute-start.79) | collective-permute-done | bytes 589856 | tf_op jit(solution)/shard_map/ppermute | solution.py:635
  576.3 10.9 %collective-permute-done.80 = bf16[1,192,768]{2,1,0:T(8,128)(2,1)S(1)} collective-permute-done((bf16[1,192,768]{2,1,0:T(8,128)(2,1)S(1)}, bf16[1,192,768]{2,1,0:T(8,128)(2,1)S(1)}, u32[]{:S(2)}, u32[]{:S(2)}) %collective-permute-start.80) | collective-permute-done | bytes 294944 | tf_op jit(solution)/shard_map/ppermute | solution.py:635
  591.9 5.3 collective-permute-done.81
  (354 shorter events, 162.4 us)
Async XLA Ops:
  7.6 29.0 %collective-permute-start.26 = (bf16[1,48,768]{2,1,0:T(8,128)(2,1)}, bf16[1,48,768]{2,1,0:T(8,128)(2,1)S(1)}, u32[]{:S(2)}, u32[]{:S(2)}) collective-permute-start(bf16[1,48,768]{2,1,0:T(8,128)(2,1)} %bitcast.99), channel_id=1, source_target_pairs={{0,16},{2,18},{4,20},{6,22},{8,24},{10,26},{12,28},{14,30},{16,0},... | collective-permute-start | bytes 221192 | tf_op jit(solution)/shard_map/ppermute | solution.py:635
  12.0 57.1 %collective-permute-start.31 = (bf16[1,4,48,768]{3,2,1,0:T(8,128)(2,1)S(1)}, bf16[1,4,48,768]{3,2,1,0:T(8,128)(2,1)S(1)}, u32[]{:S(2)}, u32[]{:S(2)}) collective-permute-start(bf16[1,4,48,768]{3,2,1,0:T(8,128)(2,1)S(1)} %bitcast.78), channel_id=1, source_target_pairs={{0,16},{2,18},{4,20},{6,22},{8,24},{10,26},{12,28},{14,30},{16,0},... | collective-permute-start | bytes 884744 | tf_op jit(solution)/shard_map/ppermute | solution.py:635
  15.0 24.7 %collective-permute-start.11 = (bf16[1,1,48,768]{3,2,1,0:T(8,128)(2,1)S(1)}, bf16[1,1,48,768]{3,2,1,0:T(8,128)(2,1)S(1)}, u32[]{:S(2)}, u32[]{:S(2)}) collective-permute-start(bf16[1,1,48,768]{3,2,1,0:T(8,128)(2,1)S(1)} %broadcast_in_dim.52), channel_id=1, source_target_pairs={{0,16},{2,18},{4,20},{6,22},{8,24},{10,26},{12,28},{14,30},{16,0},... | collective-permute-start | bytes 221192 | tf_op jit(solution)/shard_map/ppermute | solution.py:635
  35.0 42.0 %collective-permute-start.36 = (bf16[1,192,768]{2,1,0:T(8,128)(2,1)S(1)}, bf16[1,192,768]{2,1,0:T(8,128)(2,1)S(1)}, u32[]{:S(2)}, u32[]{:S(2)}) collective-permute-start(bf16[1,192,768]{2,1,0:T(8,128)(2,1)S(1)} %bitcast.87), channel_id=1, source_target_pairs={{0,16},{2,18},{4,20},{6,22},{8,24},{10,26},{12,28},{14,30},{16,0},... | collective-permute-start | bytes 884744 | tf_op jit(solution)/shard_map/ppermute | solution.py:635
  36.6 30.4 %collective-permute-start.21 = (bf16[2,1,48,768]{3,2,1,0:T(8,128)(2,1)S(1)}, bf16[2,1,48,768]{3,2,1,0:T(8,128)(2,1)S(1)}, u32[]{:S(2)}, u32[]{:S(2)}) collective-permute-start(bf16[2,1,48,768]{3,2,1,0:T(8,128)(2,1)S(1)} %bitcast.84), channel_id=1, source_target_pairs={{0,16},{2,18},{4,20},{6,22},{8,24},{10,26},{12,28},{14,30},{16,0},... | collective-permute-start | bytes 442376 | tf_op jit(solution)/shard_map/ppermute | solution.py:635
  38.0 29.0 %collective-permute-start.16 = (bf16[2,1,48,768]{3,2,1,0:T(8,128)(2,1)S(1)}, bf16[2,1,48,768]{3,2,1,0:T(8,128)(2,1)S(1)}, u32[]{:S(2)}, u32[]{:S(2)}) collective-permute-start(bf16[2,1,48,768]{3,2,1,0:T(8,128)(2,1)S(1)} %bitcast.81), channel_id=1, source_target_pairs={{0,16},{2,18},{4,20},{6,22},{8,24},{10,26},{12,28},{14,30},{16,0},... | collective-permute-start | bytes 442376 | tf_op jit(solution)/shard_map/ppermute | solution.py:635
  39.7 25.1 %collective-permute-start.3 = (bf16[16,768]{1,0:T(8,128)(2,1)S(1)}, bf16[16,768]{1,0:T(8,128)(2,1)S(1)}, u32[]{:S(2)}, u32[]{:S(2)}) collective-permute-start(bf16[16,768]{1,0:T(8,128)(2,1)S(1)} %add.246), channel_id=1, source_target_pairs={{0,16},{2,18},{4,20},{6,22},{8,24},{10,26},{12,28},{14,30},{16,0},... | collective-permute-start | bytes 73736 | tf_op jit(solution)/shard_map/ppermute | solution.py:635
  64.8 57.3 %collective-permute-start.4 = (bf16[768,768]{1,0:T(8,128)(2,1)S(1)}, bf16[768,768]{1,0:T(8,128)(2,1)S(1)}, u32[]{:S(2)}, u32[]{:S(2)}) collective-permute-start(bf16[768,768]{1,0:T(8,128)(2,1)S(1)} %copy-done.27), channel_id=1, source_target_pairs={{0,1},{1,0},{2,3},{3,2},{4,5},{5,4},{6,7},{7,6},{8,9},{9,8},{10,11... | collective-permute-start | bytes 3538952 | tf_op jit(solution)/shard_map/ppermute | solution.py:635
  76.9 30.5 %collective-permute-start.32 = (bf16[2,4,48,768]{3,2,1,0:T(8,128)(2,1)S(1)}, bf16[2,4,48,768]{3,2,1,0:T(8,128)(2,1)S(1)}, u32[]{:S(2)}, u32[]{:S(2)}) collective-permute-start(bf16[2,4,48,768]{3,2,1,0:T(8,128)(2,1)S(1)} %pad_maximum_fusion.5), channel_id=1, source_target_pairs={{0,8},{2,10},{4,12},{6,14},{8,0},{10,2},{12,4},{14,6},{16,24},{18,... | collective-permute-start | bytes 1769480 | tf_op jit(solution)/shard_map/ppermute | solution.py:635
  79.0 26.3 %collective-permute-start.17 = (bf16[2,2,48,768]{3,2,1,0:T(8,128)(2,1)S(1)}, bf16[2,2,48,768]{3,2,1,0:T(8,128)(2,1)S(1)}, u32[]{:S(2)}, u32[]{:S(2)}) collective-permute-start(bf16[2,2,48,768]{3,2,1,0:T(8,128)(2,1)S(1)} %pad_maximum_fusion.7), channel_id=1, source_target_pairs={{0,8},{2,10},{4,12},{6,14},{8,0},{10,2},{12,4},{14,6},{16,24},{18,... | collective-permute-start | bytes 884744 | tf_op jit(solution)/shard_map/ppermute | solution.py:635
  88.4 27.5 %collective-permute-start.37 = (bf16[2,192,768]{2,1,0:T(8,128)(2,1)S(1)}, bf16[2,192,768]{2,1,0:T(8,128)(2,1)S(1)}, u32[]{:S(2)}, u32[]{:S(2)}) collective-permute-start(bf16[2,192,768]{2,1,0:T(8,128)(2,1)S(1)} %pad_maximum_fusion.6), channel_id=1, source_target_pairs={{0,8},{2,10},{4,12},{6,14},{8,0},{10,2},{12,4},{14,6},{16,24},{18,... | collective-permute-start | bytes 1769480 | tf_op jit(solution)/shard_map/ppermute | solution.py:635
  119.5 41.8 %collective-permute-start.29 = (bf16[4,48,768]{2,1,0:T(8,128)(2,1)S(1)}, bf16[4,48,768]{2,1,0:T(8,128)(2,1)S(1)}, u32[]{:S(2)}, u32[]{:S(2)}) collective-permute-start(bf16[4,48,768]{2,1,0:T(8,128)(2,1)S(1)} %pad_maximum_fusion.9.refs_4_), channel_id=1, source_target_pairs={{0,2},{2,0},{4,6},{6,4},{8,10},{10,8},{12,14},{14,12},{16,18},{18,... | collective-permute-start | bytes 884744 | tf_op jit(solution)/shard_map/ppermute | solution.py:635
  119.5 59.0 %collective-permute-start.28 = (bf16[4,48,768]{2,1,0:T(8,128)(2,1)S(1)}, bf16[4,48,768]{2,1,0:T(8,128)(2,1)}, u32[]{:S(2)}, u32[]{:S(2)}) collective-permute-start(bf16[4,48,768]{2,1,0:T(8,128)(2,1)S(1)} %pad_maximum_fusion.9.refs_4_), channel_id=1, source_target_pairs={{0,4},{2,6},{4,0},{6,2},{8,12},{10,14},{12,8},{14,10},{16,20},{18,... | collective-permute-start | bytes 884744 | tf_op jit(solution)/shard_map/ppermute | solution.py:635
  133.5 30.4 %collective-permute-start.24 = (bf16[2,4,48,768]{3,2,1,0:T(8,128)(2,1)S(1)}, bf16[2,4,48,768]{3,2,1,0:T(8,128)(2,1)}, u32[]{:S(2)}, u32[]{:S(2)}) collective-permute-start(bf16[2,4,48,768]{3,2,1,0:T(8,128)(2,1)S(1)} %pad_maximum_fusion.4.refs_0_), channel_id=1, source_target_pairs={{0,2},{2,0},{4,6},{6,4},{8,10},{10,8},{12,14},{14,12},{16,18},{18,... | collective-permute-start | bytes 1769480 | tf_op jit(solution)/shard_map/ppermute | solution.py:635
  133.8 28.1 %collective-permute-start.18 = (bf16[2,4,48,768]{3,2,1,0:T(8,128)(2,1)S(1)}, bf16[2,4,48,768]{3,2,1,0:T(8,128)(2,1)}, u32[]{:S(2)}, u32[]{:S(2)}) collective-permute-start(bf16[2,4,48,768]{3,2,1,0:T(8,128)(2,1)S(1)} %pad_maximum_fusion.3.refs_0_), channel_id=1, source_target_pairs={{0,4},{2,6},{4,0},{6,2},{8,12},{10,14},{12,8},{14,10},{16,20},{18,... | collective-permute-start | bytes 1769480 | tf_op jit(solution)/shard_map/ppermute | solution.py:635
  161.9 28.8 %collective-permute-start.38 = (bf16[4,192,768]{2,1,0:T(8,128)(2,1)S(1)}, bf16[4,192,768]{2,1,0:T(8,128)(2,1)S(1)}, u32[]{:S(2)}, u32[]{:S(2)}) collective-permute-start(bf16[4,192,768]{2,1,0:T(8,128)(2,1)S(1)} %pad_maximum_fusion.1.refs_12_), channel_id=1, source_target_pairs={{0,4},{2,6},{4,0},{6,2},{8,12},{10,14},{12,8},{14,10},{16,20},{18,... | collective-permute-start | bytes 3538952 | tf_op jit(solution)/shard_map/ppermute | solution.py:635
  163.8 51.5 %collective-permute-start.33 = (bf16[4,4,48,768]{3,2,1,0:T(8,128)(2,1)S(1)}, bf16[4,4,48,768]{3,2,1,0:T(8,128)(2,1)S(1)}, u32[]{:S(2)}, u32[]{:S(2)}) collective-permute-start(bf16[4,4,48,768]{3,2,1,0:T(8,128)(2,1)S(1)} %pad_maximum_fusion.refs_8_), channel_id=1, source_target_pairs={{0,4},{2,6},{4,0},{6,2},{8,12},{10,14},{12,8},{14,10},{16,20},{18,... | collective-permute-start | bytes 3538952 | tf_op jit(solution)/shard_map/ppermute | solution.py:635
  178.5 52.0 %collective-permute-start.30 = (bf16[4,48,768]{2,1,0:T(8,128)(2,1)}, bf16[4,48,768]{2,1,0:T(8,128)(2,1)S(1)}, u32[]{:S(2)}, u32[]{:S(2)}) collective-permute-start(bf16[4,48,768]{2,1,0:T(8,128)(2,1)} %collective-permute-done.28.refs_5_), channel_id=1, source_target_pairs={{0,2},{2,0},{4,6},{6,4},{8,10},{10,8},{12,14},{14,12},{16,18},{18,... | collective-permute-start | bytes 884744 | tf_op jit(solution)/shard_map/ppermute | solution.py:635
  178.9 51.6 %collective-permute-start.39 = (bf16[4,192,768]{2,1,0:T(8,128)(2,1)S(1)}, bf16[4,192,768]{2,1,0:T(8,128)(2,1)S(1)}, u32[]{:S(2)}, u32[]{:S(2)}) collective-permute-start(bf16[4,192,768]{2,1,0:T(8,128)(2,1)S(1)} %pad_maximum_fusion.1.refs_12_), channel_id=1, source_target_pairs={{0,2},{2,0},{4,6},{6,4},{8,10},{10,8},{12,14},{14,12},{16,18},{18,... | collective-permute-start | bytes 3538952 | tf_op jit(solution)/shard_map/ppermute | solution.py:635
  179.1 51.4 %collective-permute-start.34 = (bf16[4,4,48,768]{3,2,1,0:T(8,128)(2,1)S(1)}, bf16[4,4,48,768]{3,2,1,0:T(8,128)(2,1)}, u32[]{:S(2)}, u32[]{:S(2)}) collective-permute-start(bf16[4,4,48,768]{3,2,1,0:T(8,128)(2,1)S(1)} %pad_maximum_fusion.refs_8_), channel_id=1, source_target_pairs={{0,2},{2,0},{4,6},{6,4},{8,10},{10,8},{12,14},{14,12},{16,18},{18,... | collective-permute-start | bytes 3538952 | tf_op jit(solution)/shard_map/ppermute | solution.py:635
  190.7 39.9 %collective-permute-start.40 = (bf16[4,192,768]{2,1,0:T(8,128)(2,1)S(1)}, bf16[4,192,768]{2,1,0:T(8,128)(2,1)}, u32[]{:S(2)}, u32[]{:S(2)}) collective-permute-start(bf16[4,192,768]{2,1,0:T(8,128)(2,1)S(1)} %collective-permute-done.38.refs_13_), channel_id=1, source_target_pairs={{0,2},{2,0},{4,6},{6,4},{8,10},{10,8},{12,14},{14,12},{16,18},{18,... | collective-permute-start | bytes 3538952 | tf_op jit(solution)/shard_map/ppermute | solution.py:635
  295.1 49.1 %collective-permute-start.67 = (f32[16,768]{1,0:T(8,128)S(1)}, f32[16,768]{1,0:T(8,128)S(1)}, u32[]{:S(2)}, u32[]{:S(2)}) collective-permute-start(f32[16,768]{1,0:T(8,128)S(1)} %constant_dynamic-update-slice_fusion.6), channel_id=1, source_target_pairs={{0,2},{2,0},{4,6},{6,4},{8,10},{10,8},{12,14},{14,12},{16,18},{18,... | collective-permute-start | bytes 147464 | tf_op jit(solution)/shard_map/ppermute | solution.py:635
  386.8 80.1 %collective-permute-start.57 = (bf16[2,8,48,768]{3,2,0,1:T(8,128)(2,1)}, bf16[2,8,48,768]{3,2,0,1:T(8,128)(2,1)}, u32[]{:S(2)}, u32[]{:S(2)}) collective-permute-start(bf16[2,8,48,768]{3,2,0,1:T(8,128)(2,1)} %copy.57), channel_id=1, source_target_pairs={{0,2},{2,0},{4,6},{6,4},{8,10},{10,8},{12,14},{14,12},{16,18},{18,... | collective-permute-start | bytes 3538952 | tf_op jit(solution)/shard_map/ppermute | solution.py:635
  386.8 81.9 %collective-permute-start.52 = (bf16[2,8,48,768]{3,2,0,1:T(8,128)(2,1)}, bf16[2,8,48,768]{3,2,0,1:T(8,128)(2,1)}, u32[]{:S(2)}, u32[]{:S(2)}) collective-permute-start(bf16[2,8,48,768]{3,2,0,1:T(8,128)(2,1)} %copy.54), channel_id=1, source_target_pairs={{0,2},{2,0},{4,6},{6,4},{8,10},{10,8},{12,14},{14,12},{16,18},{18,... | collective-permute-start | bytes 3538952 | tf_op jit(solution)/shard_map/ppermute | solution.py:635
  394.4 77.5 %collective-permute-start.41 = (bf16[768,768]{1,0:T(8,128)(2,1)S(1)}, bf16[768,768]{1,0:T(8,128)(2,1)S(1)}, u32[]{:S(2)}, u32[]{:S(2)}) collective-permute-start(bf16[768,768]{1,0:T(8,128)(2,1)S(1)} %convert_element_type.92), channel_id=1, source_target_pairs={{0,1},{1,0},{2,3},{3,2},{4,5},{5,4},{6,7},{7,6},{8,9},{9,8},{10,11... | collective-permute-start | bytes 3538952 | tf_op jit(solution)/shard_map/ppermute | solution.py:635
  413.6 86.0 %collective-permute-start.72 = (bf16[8,4,48,768]{3,2,1,0:T(8,128)(2,1)S(1)}, bf16[8,4,48,768]{3,2,1,0:T(8,128)(2,1)S(1)}, u32[]{:S(2)}, u32[]{:S(2)}) collective-permute-start(bf16[8,4,48,768]{3,2,1,0:T(8,128)(2,1)S(1)} %copy-done.25), channel_id=1, source_target_pairs={{0,2},{2,0},{4,6},{6,4},{8,10},{10,8},{12,14},{14,12},{16,18},{18,... | collective-permute-start | bytes 7077896 | tf_op jit(solution)/shard_map/ppermute | solution.py:635
  466.2 34.0 %collective-permute-start.77 = (bf16[8,192,768]{2,1,0:T(8,128)(2,1)S(1)}, bf16[8,192,768]{2,1,0:T(8,128)(2,1)S(1)}, u32[]{:S(2)}, u32[]{:S(2)}) collective-permute-start(bf16[8,192,768]{2,1,0:T(8,128)(2,1)S(1)} %copy-done.24), channel_id=1, source_target_pairs={{0,2},{2,0},{4,6},{6,4},{8,10},{10,8},{12,14},{14,12},{16,18},{18,... | collective-permute-start | bytes 7077896 | tf_op jit(solution)/shard_map/ppermute | solution.py:635
  470.2 26.5 %collective-permute-start.53 = (bf16[2,4,48,768]{3,2,0,1:T(8,128)(2,1)S(1)}, bf16[2,4,48,768]{3,2,0,1:T(8,128)(2,1)S(1)}, u32[]{:S(2)}, u32[]{:S(2)}) collective-permute-start(bf16[2,4,48,768]{3,2,0,1:T(8,128)(2,1)S(1)} %get-tuple-element.153), channel_id=1, source_target_pairs={{0,4},{2,6},{4,0},{6,2},{8,12},{10,14},{12,8},{14,10},{16,20},{18,... | collective-permute-start | bytes 1769480 | tf_op jit(solution)/shard_map/ppermute | solution.py:635
  499.8 29.0 %collective-permute-start.73 = (bf16[4,4,48,768]{3,2,1,0:T(8,128)(2,1)S(1)}, bf16[4,4,48,768]{3,2,1,0:T(8,128)(2,1)S(1)}, u32[]{:S(2)}, u32[]{:S(2)}) collective-permute-start(bf16[4,4,48,768]{3,2,1,0:T(8,128)(2,1)S(1)} %get-tuple-element.137), channel_id=1, source_target_pairs={{0,4},{2,6},{4,0},{6,2},{8,12},{10,14},{12,8},{14,10},{16,20},{18,... | collective-permute-start | bytes 3538952 | tf_op jit(solution)/shard_map/ppermute | solution.py:635
  501.5 50.7 %collective-permute-start.78 = (bf16[4,192,768]{2,1,0:T(8,128)(2,1)S(1)}, bf16[4,192,768]{2,1,0:T(8,128)(2,1)S(1)}, u32[]{:S(2)}, u32[]{:S(2)}) collective-permute-start(bf16[4,192,768]{2,1,0:T(8,128)(2,1)S(1)} %get-tuple-element.135), channel_id=1, source_target_pairs={{0,4},{2,6},{4,0},{6,2},{8,12},{10,14},{12,8},{14,10},{16,20},{18,... | collective-permute-start | bytes 3538952 | tf_op jit(solution)/shard_map/ppermute | solution.py:635
  517.0 36.5 %collective-permute-start.56 = (bf16[2,48,768]{2,1,0:T(8,128)(2,1)S(1)}, bf16[2,48,768]{2,1,0:T(8,128)(2,1)S(1)}, u32[]{:S(2)}, u32[]{:S(2)}) collective-permute-start(bf16[2,48,768]{2,1,0:T(8,128)(2,1)S(1)} %fusion.17), channel_id=1, source_target_pairs={{0,1},{1,0},{2,3},{3,2},{4,5},{5,4},{6,7},{7,6},{8,9},{9,8},{10,11... | collective-permute-start | bytes 442376 | tf_op jit(solution)/shard_map/ppermute | solution.py:635
  529.7 24.0 %collective-permute-start.74 = (bf16[2,4,48,768]{3,2,1,0:T(8,128)(2,1)}, bf16[2,4,48,768]{3,2,1,0:T(8,128)(2,1)}, u32[]{:S(2)}, u32[]{:S(2)}) collective-permute-start(bf16[2,4,48,768]{3,2,1,0:T(8,128)(2,1)} %get-tuple-element.141), channel_id=1, source_target_pairs={{0,8},{2,10},{4,12},{6,14},{8,0},{10,2},{12,4},{14,6},{16,24},{18,... | collective-permute-start | bytes 1769480 | tf_op jit(solution)/shard_map/ppermute | solution.py:635
  (91 other events, 1248.1 us)
